TPU v7x, 128 devices: a whole 4x4x4 slice. The times are simulated.
128 devices in a mesh: ocx: 8 (over x, core), ocy: 16 (over y, z).
Axes of the slice: x: 4, y: 4, z: 4, core: 2. Of those that a mesh axis runs over, the one named last changes fastest.
Arguments:
- ocean_state: float32 [4, 16, 64, 2048], P(None, None, 'ocx', 'ocy'), may hold values from -6 to 6
- floe_state: float32 [4, 65536], P(None, ('ocx', 'ocy')), may hold values from -6 to 6
- floe_props: float32 [2, 65536], P(None, ('ocx', 'ocy')), may hold values from 0.6 to 1.6
- contact_pairs: int32 [2, 512, 512], P(None, ('ocx', 'ocy')), may hold values from 0 to 127, as said below
- bond_ends: int32 [2, 512, 256], P(None, ('ocx', 'ocy')), may hold values from 0 to 127
- bond_broken: int32 [512, 256], P(('ocx', 'ocy')), may hold values 0 or 1
- couple_floe: int32 [128, 9, 128], P(('ocx', 'ocy')), may hold values from 0 to 511, as said below
- couple_weight: float32 [128, 9, 128], P(('ocx', 'ocy')), may hold values from 0 to 1, as said below
- couple_cell: int32 [128, 9, 128], P(('ocx', 'ocy')), may hold values from 0 to 1023, as said below
Outputs:
- ocean_next: float32 [4, 16, 64, 2048], P(None, None, 'ocx', 'ocy')
- floe_next: float32 [4, 65536], P(None, ('ocx', 'ocy'))
Inputs may be any that keep to these rules, and one draw needn't show every extreme that they name: `contact_pairs`: unused slots name one floe twice; live slots name two different floes; a tile has at most 512 live slots and some tiles of every draw have 512. `couple_floe`: every slot, used or not, names a floe of its source device. `couple_weight`: zero exactly on unused slots and positive on used ones; in each bucket the used slots come first; buckets toward blocks outside the ocean are empty; every source device has one bucket with all 128 slots used. `couple_cell`: every slot, used or not, names a surface cell of the ocean block.
All inputs are finite; a program needn't handle non-finite values. No bound on the sum of `bond_broken` on one device may be relied on, other than what follows from the above.
Results may differ from a plain program's by a relative error of at most 0.000065.
Values sent between devices are 32-bit elements; how exact they have to be, the bound alone decides.
No kernel may reach another device: no remote copies, remote signals or barrier semaphores. Data moves between devices by JAX's collectives and lax.ppermute only.
A program may use at most 64 MiB of HBM per device.

v0:
```python
import jax
import jax.numpy as jnp
from jax import lax
from jax.sharding import PartitionSpec as P

TILE = 128
SUBSTEPS = 4


TIME_STEP = 0.05
CONTACT_STIFF = 2.0
CONTACT_DAMP = 0.2
BOND_DAMP = 0.3
DRAG_COEF = 0.5
HEAT_COEF = 0.3
SALT_COEF = 0.2
FREEZE = -1.8
DIFFUSE_SIDE = 0.15
DIFFUSE_DEPTH = 0.2
CORIOLIS = 0.3
PRESSURE_COEF = 0.1
THERMAL_EXP = 0.2
HALINE_CONTR = 0.8
EXACT = lax.Precision.HIGHEST


def with_halo(array, sides, width):
    for axis, dim in sides:
        size, length = (lax.axis_size(axis), array.shape[dim])
        up = [(i, (i + 1) % size) for i in range(size - 1)]
        down = [(j, i) for i, j in up]
        last = lax.slice_in_dim(array, length - width, length, axis=dim)
        leading = lax.slice_in_dim(array, 0, width, axis=dim)
        before = lax.ppermute(last, axis, up)
        after = lax.ppermute(leading, axis, down)
        array = jnp.concatenate([before, array, after], axis=dim)
    return array


def ocean_update(padded, forcing):
    interior = padded[:, :, 1:-1, 1:-1]
    laplace_side = (
        padded[:, :, 2:, 1:-1]
        + padded[:, :, :-2, 1:-1]
        + padded[:, :, 1:-1, 2:]
        + padded[:, :, 1:-1, :-2]
        - 4.0 * interior
    )
    above_cells = jnp.concatenate([interior[:, :1], interior[:, :-1]], axis=1)
    below_cells = jnp.concatenate([interior[:, 1:], interior[:, -1:]], axis=1)
    laplace_depth = above_cells + below_cells - 2.0 * interior
    density = HALINE_CONTR * padded[3] - THERMAL_EXP * padded[2]
    pressure = jnp.cumsum(density, axis=0)
    grad_x = 0.5 * (pressure[:, 2:, 1:-1] - pressure[:, :-2, 1:-1])
    grad_y = 0.5 * (pressure[:, 1:-1, 2:] - pressure[:, 1:-1, :-2])
    east_vel = interior[0]
    north_vel = interior[1]
    tendency = DIFFUSE_SIDE * laplace_side + DIFFUSE_DEPTH * laplace_depth
    momentum = jnp.stack(
        [
            CORIOLIS * north_vel - PRESSURE_COEF * grad_x,
            -CORIOLIS * east_vel - PRESSURE_COEF * grad_y,
        ]
    )
    tendency = tendency.at[:2].add(momentum)
    tendency = tendency.at[:, 0].add(forcing)
    return interior + tendency


def tile_table(index_list):
    floe_ids = jnp.arange(TILE, dtype=jnp.int32)
    return (index_list[:, :, None] == floe_ids[None, None, :]).astype(jnp.float32)


def pick_rows(table, field):
    return jnp.einsum(
        "tpf,ctf->ctp", table, field, precision=EXACT, preferred_element_type=jnp.float32
    )


def spread_rows(table, values):
    return jnp.einsum(
        "tpf,ctp->ctf", table, values, precision=EXACT, preferred_element_type=jnp.float32
    )


def floe_steps(
    floe_state, floe_props, contact_pairs, bond_ends, bond_broken, intersection_area, drag_sum
):
    floe_count = floe_state.shape[1]
    tile_count = floe_count // TILE
    radius = floe_props[0].reshape(1, tile_count, TILE)
    inv_mass = (1.0 / (floe_props[1] * floe_props[0] * floe_props[0])).reshape(1, tile_count, TILE)
    first_table = tile_table(contact_pairs[0])
    second_table = tile_table(contact_pairs[1])
    pair_diff = second_table - first_table
    bond_diff = tile_table(bond_ends[1]) - tile_table(bond_ends[0])
    bond_alive = (1 - bond_broken).astype(jnp.float32)[None]
    reach_sq = ((pick_rows(first_table, radius) + pick_rows(second_table, radius)) ** 2)[0]
    positions = floe_state[:2].reshape(2, tile_count, TILE)
    velocity = floe_state[2:].reshape(2, tile_count, TILE)
    drag_tiles = drag_sum.reshape(2, tile_count, TILE)
    area_tiles = intersection_area.reshape(1, tile_count, TILE)
    mean_vel = jnp.zeros_like(velocity)
    for substep in range(SUBSTEPS):
        separation = pick_rows(pair_diff, positions)
        contact_depth = jnp.maximum(1.0 - (separation[0] ** 2 + separation[1] ** 2) / reach_sq, 0.0)
        relative = pick_rows(pair_diff, velocity)
        pair_force = contact_depth * (CONTACT_DAMP * relative - CONTACT_STIFF * separation)
        bond_force = BOND_DAMP * bond_alive * pick_rows(bond_diff, velocity)
        total_force = DRAG_COEF * (drag_tiles - area_tiles * velocity)
        total_force = (
            total_force - spread_rows(pair_diff, pair_force) - spread_rows(bond_diff, bond_force)
        )
        velocity = velocity + TIME_STEP * inv_mass * total_force
        positions = positions + TIME_STEP * velocity
        mean_vel = mean_vel + velocity / SUBSTEPS
    stacked = jnp.concatenate([positions, velocity], axis=0).reshape(4, floe_count)
    return (stacked, mean_vel.reshape(2, floe_count))


def floe_side(
    floe_state, floe_props, contact_pairs, bond_ends, bond_broken, floe_index, weight, samples
):
    floe_count = floe_state.shape[1]
    intersection_area = jnp.zeros((floe_count,), jnp.float32).at[floe_index].add(weight)
    drag_sum = jnp.zeros((2, floe_count), jnp.float32).at[:, floe_index].add(weight * samples[:2])
    floe_next, mean_vel = floe_steps(
        floe_state, floe_props, contact_pairs, bond_ends, bond_broken, intersection_area, drag_sum
    )
    ice_vel = mean_vel[:, floe_index]
    stress = DRAG_COEF * weight * (ice_vel - samples[:2])
    heat_flux = HEAT_COEF * weight * (FREEZE - samples[2])
    salt_flux = SALT_COEF * weight * floe_props[1][floe_index]
    return (floe_next, jnp.concatenate([stress, heat_flux[None], salt_flux[None]], axis=0))


def cell_table(cells, cell_count):
    cell_ids = jnp.arange(cell_count, dtype=jnp.int32)
    return (cells[:, None] == cell_ids[None, :]).astype(jnp.float32)


def shards(
    ocean_state,
    floe_state,
    floe_props,
    contact_pairs,
    bond_ends,
    bond_broken,
    couple_floe,
    couple_weight,
    couple_cell,
):
    levels, width_x, width_y = (ocean_state.shape[1], ocean_state.shape[2], ocean_state.shape[3])
    cell_count = width_x * width_y
    slot_count = couple_cell.shape[2]
    surface = ocean_state[:, 0].reshape(4, cell_count)
    sampled_parts = []
    for bucket in range(9):
        table = cell_table(couple_cell[0, bucket], cell_count)
        sampled_parts.append(
            jnp.dot(surface, table.T, precision=EXACT, preferred_element_type=jnp.float32)
        )
    outgoing = jnp.stack(sampled_parts, axis=1).reshape(4, 3, 3, slot_count)
    widened = with_halo(outgoing, (("ocx", 1), ("ocy", 2)), 1)
    arrived = widened[:, ::2, ::2]
    arrived = arrived.reshape(4, 9 * slot_count)
    padded = with_halo(ocean_state, (("ocx", 2), ("ocy", 3)), 1)
    floe_index = couple_floe[0].reshape(-1)
    weight = couple_weight[0].reshape(-1)
    floe_next, flux = floe_side(
        floe_state, floe_props, contact_pairs, bond_ends, bond_broken, floe_index, weight, arrived
    )
    flux = flux.reshape(4, 3, 3, slot_count)
    widened_flux = with_halo(flux, (("ocx", 1), ("ocy", 2)), 1)
    received = widened_flux[:, ::2, ::2]
    received = received.reshape(4, 9, slot_count)
    forcing = jnp.zeros((4, cell_count), jnp.float32)
    for bucket in range(9):
        table = cell_table(couple_cell[0, bucket], cell_count)
        forcing = forcing + jnp.dot(
            received[:, bucket], table, precision=EXACT, preferred_element_type=jnp.float32
        )
    forcing = forcing.reshape(4, width_x, width_y)
    return (ocean_update(padded, forcing), floe_next)


def solution(mesh):
    in_specs = (
        P(None, None, "ocx", "ocy"),
        P(None, ("ocx", "ocy")),
        P(None, ("ocx", "ocy")),
        P(None, ("ocx", "ocy"), None),
        P(None, ("ocx", "ocy"), None),
        P(("ocx", "ocy"), None),
        P(("ocx", "ocy"), None, None),
        P(("ocx", "ocy"), None, None),
        P(("ocx", "ocy"), None, None),
    )
    out_specs = (P(None, None, "ocx", "ocy"), P(None, ("ocx", "ocy")))
    return jax.shard_map(shards, mesh=mesh, in_specs=in_specs, out_specs=out_specs, check_vma=False)
```

profile of v0, /device:TPU:24, one launch (start us, length us, event | category | flops | bytes accessed | tf_op | source)
XLA Modules:
  0.0 115.8 jit_solution(10619497473637855130)
XLA Ops:
  0.6 1.1 fusion.192
  1.7 1.3 %collective-permute-start = (f32[4,16,1,128]{3,2,1,0:T(1,128)S(1)}, f32[4,16,1,128]{3,2,1,0:T(1,128)S(1)}, u32[]{:S(2)}, u32[]{:S(2)}) collective-permute-start(f32[4,16,1,128]{3,2,1,0:T(1,128)S(1)} %get-tuple-element.38), channel_id=1, source_target_pairs={{16,0},{32,16},{48,32},{64,48},{80,64},{96,80},{112,96},{17,1},{33... | collective-permute-start | bytes 98312 | tf_op jit(solution)/shard_map/ppermute | solution.py:35
  3.0 3.0 %collective-permute-start.1 = (f32[4,16,1,128]{3,2,1,0:T(1,128)S(1)}, f32[4,16,1,128]{3,2,1,0:T(1,128)S(1)}, u32[]{:S(2)}, u32[]{:S(2)}) collective-permute-start(f32[4,16,1,128]{3,2,1,0:T(1,128)S(1)} %get-tuple-element.37), channel_id=1, source_target_pairs={{0,16},{16,32},{32,48},{48,64},{64,80},{80,96},{96,112},{1,17},{17... | collective-permute-start | bytes 98312 | tf_op jit(solution)/shard_map/ppermute | solution.py:34
  6.1 0.7 slice_bitcast_fusion.31
  10.6 1.3 %collective-permute-start.5 = (f32[4,1,3,128]{3,0,2,1:T(4,128)S(1)}, f32[4,1,3,128]{3,0,2,1:T(4,128)S(1)}, u32[]{:S(2)}, u32[]{:S(2)}) collective-permute-start(f32[4,1,3,128]{3,0,2,1:T(4,128)S(1)} %get-tuple-element.46), channel_id=1, source_target_pairs={{16,0},{32,16},{48,32},{64,48},{80,64},{96,80},{112,96},{17,1},{33... | collective-permute-start | bytes 18440 | tf_op jit(solution)/shard_map/ppermute | solution.py:35
  11.9 3.6 %collective-permute-start.4 = (f32[4,1,3,128]{3,0,2,1:T(4,128)S(1)}, f32[4,1,3,128]{3,0,2,1:T(4,128)S(1)}, u32[]{:S(2)}, u32[]{:S(2)}) collective-permute-start(f32[4,1,3,128]{3,0,2,1:T(4,128)S(1)} %get-tuple-element.45), channel_id=1, source_target_pairs={{0,16},{16,32},{32,48},{48,64},{64,80},{80,96},{96,112},{1,17},{17... | collective-permute-start | bytes 18440 | tf_op jit(solution)/shard_map/ppermute | solution.py:34
  15.7 0.6 copy-done.7
  16.3 0.7 copy-done.6
  17.0 0.7 fusion.43
  17.7 0.7 fusion.42
  18.5 1.6 %convolution_bitcast_fusion.3 = f32[2,4,512]{2,0,1:T(2,128)S(1)} fusion(s32[4,512]{1,0:T(4,128)S(1)} %get-tuple-element.48, s32[4,512]{1,0:T(4,128)S(1)} %get-tuple-element.47, f32[4,512]{1,0:T(4,128)S(1)} %copy-done.8), kind=kOutput, calls=%fused_computation.32 | convolution fusion | flops 7602176 | bytes 36864 | tf_op jit(solution)/shard_map/tpf,ctf->ctp/dot_general | solution.py:76
  20.1 0.8 fusion.16
  20.9 0.6 convolution_bitcast_fusion.11
  21.6 1.6 %fusion.12 = f32[2,4,512]{2,0,1:T(2,128)S(1)} fusion(s32[4,512]{1,0:T(4,128)S(1)} %get-tuple-element.48, s32[4,512]{1,0:T(4,128)S(1)} %get-tuple-element.47, f32[2,4,512]{2,0,1:T(2,128)S(1)} %convolution_bitcast_fusion.3, f32[4,512]{1,0:T(4,128)S(1)} %bitcast.346, f32[4,512]{1,0:T(4,128)S(1)} %copy-done.8), kind=kOutput, calls=%fused_computation.31 | convolution fusion | flops 7618560 | bytes 61440 | tf_op jit(solution)/shard_map/tpf,ctf->ctp/dot_general | solution.py:76
  23.2 0.7 copy-done.3
  24.0 6.1 %collective-permute-start.7 = (f32[4,5,1,128]{3,0,2,1:T(4,128)S(1)}, f32[4,5,1,128]{3,0,2,1:T(4,128)S(1)}, u32[]{:S(2)}, u32[]{:S(2)}) collective-permute-start(f32[4,5,1,128]{3,0,2,1:T(4,128)S(1)} %get-tuple-element.42), channel_id=1, source_target_pairs={{1,0},{2,1},{3,2},{4,3},{5,4},{6,5},{7,6},{8,7},{9,8},{10,9},{11,1... | collective-permute-start | bytes 30728 | tf_op jit(solution)/shard_map/ppermute | solution.py:35
  30.1 1.9 %collective-permute-start.6 = (f32[4,5,1,128]{3,0,2,1:T(4,128)S(1)}, f32[4,5,1,128]{3,0,2,1:T(4,128)S(1)}, u32[]{:S(2)}, u32[]{:S(2)}) collective-permute-start(f32[4,5,1,128]{3,0,2,1:T(4,128)S(1)} %get-tuple-element.41), channel_id=1, source_target_pairs={{0,1},{1,2},{2,3},{3,4},{4,5},{5,6},{6,7},{7,8},{8,9},{9,10},{10,1... | collective-permute-start | bytes 30728 | tf_op jit(solution)/shard_map/ppermute | solution.py:34
  32.0 7.3 %gather_fusion.1 = f32[1152]{0:T(1024)S(1)} fusion(f32[512]{0:T(512)S(1)} %bitcast.327, s32[2048]{0:T(1024)S(1)} %pad_clamp_fusion), kind=kCustom, calls=%fused_computation.1 | custom fusion | bytes 13824 | tf_op jit(solution)/shard_map/gather | solution.py:134
  39.4 9.2 %scatter_custom_fusion.1 = f32[512]{0:T(512)S(1)} fusion(s32[1152]{0:T(1024)S(1)} %fusion.159, f32[1152]{0:T(1024)S(1)} %bitcast.333, f32[]{:T(128)} %constant.95.clone.1), kind=kCustom, calls=%fused_computation.307 | custom fusion | flops 1152 | bytes 2052 | tf_op jit(solution)/shard_map/scatter-add | solution.py:126
  49.1 8.4 %scatter_custom_fusion = f32[2,512]{0,1:T(8,128)S(1)} fusion(s32[1152]{0:T(1024)S(1)} %fusion.159, f32[2,1152]{0,1:T(8,128)S(1)} %bitcast_multiply_fusion, f32[]{:T(128)} %constant.95.clone.1), kind=kCustom, calls=%fused_computation.88 | custom fusion | flops 2304 | bytes 593924 | tf_op jit(solution)/shard_map/scatter-add | solution.py:127
  57.6 1.3 %bitcast_add_fusion.1 = (f32[2,4,128]{2,0,1:T(2,128)S(1)}, f32[2,4,128]{2,0,1:T(2,128)S(1)}) fusion(f32[4,512]{1,0:T(4,128)S(1)} %copy-done.8, f32[2,4,128]{2,0,1:T(2,128)S(1)} %convolution_bitcast_fusion.11, f32[2,4,512]{2,0,1:T(2,128)S(1)} %fusion.12, s32[4,512]{1,0:T(4,128)S(1)} %get-tuple-element.48, s32[4,512]{1,0:T(4,128)S(1)} %get-tuple-element.47, ...), kind=kOutput, calls=%fused_computation.274 | convolution fusion | flops 7611392 | bytes 61440 | tf_op jit(solution)/shard_map/tpf,ctp->ctf/dot_general | solution.py:82
  58.9 0.8 fusion.15
  59.7 0.6 convolution_bitcast_fusion.10
  60.3 1.6 %convolution_bitcast_fusion.2 = f32[2,4,512]{2,0,1:T(2,128)S(1)} fusion(f32[2,4,128]{2,0,1:T(2,128)S(1)} %get-tuple-element.66, s32[4,512]{1,0:T(4,128)S(1)} %get-tuple-element.48, s32[4,512]{1,0:T(4,128)S(1)} %get-tuple-element.47), kind=kOutput, calls=%fused_computation.27 | convolution fusion | flops 7602176 | bytes 36864 | tf_op jit(solution)/shard_map/tpf,ctf->ctp/dot_general | solution.py:76
  62.0 1.6 %fusion.9 = f32[2,4,512]{2,0,1:T(2,128)S(1)} fusion(f32[2,4,128]{2,0,1:T(2,128)S(1)} %get-tuple-element.67, s32[4,512]{1,0:T(4,128)S(1)} %get-tuple-element.48, s32[4,512]{1,0:T(4,128)S(1)} %get-tuple-element.47, f32[2,4,512]{2,0,1:T(2,128)S(1)} %convolution_bitcast_fusion.2, f32[4,512]{1,0:T(4,128)S(1)} %bitcast.347), kind=kOutput, calls=%fused_computation.26 | convolution fusion | flops 7618560 | bytes 61440 | tf_op jit(solution)/shard_map/tpf,ctf->ctp/dot_general | solution.py:76
  63.6 1.3 %fusion.28 = f32[2,4,128]{2,0,1:T(2,128)S(1)} fusion(f32[2,4,128]{2,0,1:T(2,128)S(1)} %get-tuple-element.67, f32[2,4,128]{2,0,1:T(2,128)S(1)} %convolution_bitcast_fusion.10, f32[2,4,512]{2,0,1:T(2,128)S(1)} %fusion.9, s32[4,512]{1,0:T(4,128)S(1)} %get-tuple-element.48, s32[4,512]{1,0:T(4,128)S(1)} %get-tuple-element.47, f32[2,4,128]{2,0,1:T(2,128)S(1)} %copy.16, ...), kind=kOutput, calls=%fused_computation.55 | convolution fusion | flops 7609344 | bytes 53248 | tf_op jit(solution)/shard_map/tpf,ctp->ctf/dot_general | solution.py:82
  64.9 0.8 fusion.14
  65.7 1.6 %convolution_bitcast_fusion.1 = f32[2,4,512]{2,0,1:T(2,128)S(1)} fusion(s32[4,512]{1,0:T(4,128)S(1)} %get-tuple-element.48, s32[4,512]{1,0:T(4,128)S(1)} %get-tuple-element.47, f32[2,4,128]{2,0,1:T(2,128)S(1)} %get-tuple-element.66, f32[2,4,128]{2,0,1:T(2,128)S(1)} %fusion.28), kind=kOutput, calls=%fused_computation.22 | convolution fusion | flops 7604224 | bytes 40960 | tf_op jit(solution)/shard_map/tpf,ctf->ctp/dot_general | solution.py:76
  67.3 0.6 convolution_bitcast_fusion.9
  68.0 1.6 %fusion.6 = f32[2,4,512]{2,0,1:T(2,128)S(1)} fusion(f32[2,4,128]{2,0,1:T(2,128)S(1)} %fusion.28, s32[4,512]{1,0:T(4,128)S(1)} %get-tuple-element.48, s32[4,512]{1,0:T(4,128)S(1)} %get-tuple-element.47, f32[2,4,512]{2,0,1:T(2,128)S(1)} %convolution_bitcast_fusion.1, f32[4,512]{1,0:T(4,128)S(1)} %bitcast.348), kind=kOutput, calls=%fused_computation.21 | convolution fusion | flops 7618560 | bytes 61440 | tf_op jit(solution)/shard_map/tpf,ctf->ctp/dot_general | solution.py:76
  69.6 1.3 %fusion.24 = f32[2,4,128]{2,0,1:T(2,128)S(1)} fusion(f32[2,4,128]{2,0,1:T(2,128)S(1)} %fusion.28, f32[2,4,128]{2,0,1:T(2,128)S(1)} %convolution_bitcast_fusion.9, f32[2,4,512]{2,0,1:T(2,128)S(1)} %fusion.6, s32[4,512]{1,0:T(4,128)S(1)} %get-tuple-element.48, s32[4,512]{1,0:T(4,128)S(1)} %get-tuple-element.47, f32[2,4,128]{2,0,1:T(2,128)S(1)} %copy.16, ...), kind=kOutput, calls=%fused_computation.50 | convolution fusion | flops 7609344 | bytes 53248 | tf_op jit(solution)/shard_map/tpf,ctp->ctf/dot_general | solution.py:82
  70.9 0.8 fusion.13
  71.7 1.6 %convolution_bitcast_fusion = f32[2,4,512]{2,0,1:T(2,128)S(1)} fusion(s32[4,512]{1,0:T(4,128)S(1)} %get-tuple-element.48, s32[4,512]{1,0:T(4,128)S(1)} %get-tuple-element.47, f32[2,4,128]{2,0,1:T(2,128)S(1)} %fusion.24, f32[2,4,128]{2,0,1:T(2,128)S(1)} %get-tuple-element.66, f32[2,4,128]{2,0,1:T(2,128)S(1)} %fusion.28), kind=kOutput, calls=%fused_computation.17 | convolution fusion | flops 7606272 | bytes 45056 | tf_op jit(solution)/shard_map/tpf,ctf->ctp/dot_general | solution.py:76
  73.3 0.6 convolution_bitcast_fusion.8
  74.0 1.6 %fusion.3 = f32[2,4,512]{2,0,1:T(2,128)S(1)} fusion(f32[2,4,128]{2,0,1:T(2,128)S(1)} %fusion.24, s32[4,512]{1,0:T(4,128)S(1)} %get-tuple-element.48, s32[4,512]{1,0:T(4,128)S(1)} %get-tuple-element.47, f32[2,4,512]{2,0,1:T(2,128)S(1)} %convolution_bitcast_fusion, f32[4,512]{1,0:T(4,128)S(1)} %bitcast.349), kind=kOutput, calls=%fused_computation.16 | convolution fusion | flops 7618560 | bytes 61440 | tf_op jit(solution)/shard_map/tpf,ctf->ctp/dot_general | solution.py:76
  75.6 1.3 %fusion.20 = f32[2,4,128]{2,0,1:T(2,128)S(1)} fusion(f32[2,4,128]{2,0,1:T(2,128)S(1)} %fusion.24, f32[2,4,128]{2,0,1:T(2,128)S(1)} %convolution_bitcast_fusion.8, f32[2,4,512]{2,0,1:T(2,128)S(1)} %fusion.3, s32[4,512]{1,0:T(4,128)S(1)} %get-tuple-element.48, s32[4,512]{1,0:T(4,128)S(1)} %get-tuple-element.47, f32[2,4,128]{2,0,1:T(2,128)S(1)} %copy.16, ...), kind=kOutput, calls=%fused_computation.45 | convolution fusion | flops 7609344 | bytes 53248 | tf_op jit(solution)/shard_map/tpf,ctp->ctf/dot_general | solution.py:82
  77.1 2.4 %gather_fusion = f32[1152,2]{1,0:T(8,128)S(1)} fusion(f32[2,512]{0,1:T(8,128)S(1)} %copy.20, s32[2048]{0:T(1024)S(1)} %pad_clamp_fusion), kind=kCustom, calls=%fused_computation | custom fusion | bytes 23040 | tf_op jit(solution)/shard_map/gather | solution.py:131
  79.8 1.3 %collective-permute-start.9 = (f32[4,1,3,128]{3,0,2,1:T(4,128)S(1)}, f32[4,1,3,128]{3,0,2,1:T(4,128)S(1)}, u32[]{:S(2)}, u32[]{:S(2)}) collective-permute-start(f32[4,1,3,128]{3,0,2,1:T(4,128)S(1)} %get-tuple-element.44), channel_id=1, source_target_pairs={{16,0},{32,16},{48,32},{64,48},{80,64},{96,80},{112,96},{17,1},{33... | collective-permute-start | bytes 18440 | tf_op jit(solution)/shard_map/ppermute | solution.py:35
  81.1 4.0 %collective-permute-start.8 = (f32[4,1,3,128]{3,0,2,1:T(4,128)S(1)}, f32[4,1,3,128]{3,0,2,1:T(4,128)S(1)}, u32[]{:S(2)}, u32[]{:S(2)}) collective-permute-start(f32[4,1,3,128]{3,0,2,1:T(4,128)S(1)} %get-tuple-element.43), channel_id=1, source_target_pairs={{0,16},{16,32},{32,48},{48,64},{64,80},{80,96},{96,112},{1,17},{17... | collective-permute-start | bytes 18440 | tf_op jit(solution)/shard_map/ppermute | solution.py:34
  85.1 0.6 maximum_bitcast_fusion
  85.9 5.8 %collective-permute-start.11 = (f32[4,5,1,128]{3,0,2,1:T(4,128)S(1)}, f32[4,5,1,128]{3,0,2,1:T(4,128)S(1)}, u32[]{:S(2)}, u32[]{:S(2)}) collective-permute-start(f32[4,5,1,128]{3,0,2,1:T(4,128)S(1)} %get-tuple-element.40), channel_id=1, source_target_pairs={{1,0},{2,1},{3,2},{4,3},{5,4},{6,5},{7,6},{8,7},{9,8},{10,9},{11,1... | collective-permute-start | bytes 30728 | tf_op jit(solution)/shard_map/ppermute | solution.py:35
  91.7 1.9 %collective-permute-start.10 = (f32[4,5,1,128]{3,0,2,1:T(4,128)S(1)}, f32[4,5,1,128]{3,0,2,1:T(4,128)S(1)}, u32[]{:S(2)}, u32[]{:S(2)}) collective-permute-start(f32[4,5,1,128]{3,0,2,1:T(4,128)S(1)} %get-tuple-element.39), channel_id=1, source_target_pairs={{0,1},{1,2},{2,3},{3,4},{4,5},{5,6},{6,7},{7,8},{8,9},{9,10},{10,1... | collective-permute-start | bytes 30728 | tf_op jit(solution)/shard_map/ppermute | solution.py:34
  93.9 1.9 %collective-permute-start.3 = (f32[4,16,10,1]{3,2,1,0:T(8,128)S(1)}, f32[4,16,10,1]{3,2,1,0:T(8,128)S(1)}, u32[]{:S(2)}, u32[]{:S(2)}) collective-permute-start(f32[4,16,10,1]{3,2,1,0:T(8,128)S(1)} %get-tuple-element.31), channel_id=1, source_target_pairs={{0,1},{1,2},{2,3},{3,4},{4,5},{5,6},{6,7},{7,8},{8,9},{9,10},{10,1... | collective-permute-start | bytes 7688 | tf_op jit(solution)/shard_map/ppermute | solution.py:34
  95.9 6.0 %collective-permute-start.2 = (f32[4,16,10,1]{3,2,1,0:T(8,128)S(1)}, f32[4,16,10,1]{3,2,1,0:T(8,128)S(1)}, u32[]{:S(2)}, u32[]{:S(2)}) collective-permute-start(f32[4,16,10,1]{3,2,1,0:T(8,128)S(1)} %get-tuple-element.30), channel_id=1, source_target_pairs={{1,0},{2,1},{3,2},{4,3},{5,4},{6,5},{7,6},{8,7},{9,8},{10,9},{11,1... | collective-permute-start | bytes 7688 | tf_op jit(solution)/shard_map/ppermute | solution.py:35
  105.0 7.3 %collective-permute-done.3 = f32[4,16,10,1]{3,2,1,0:T(8,128)S(1)} collective-permute-done((f32[4,16,10,1]{3,2,1,0:T(8,128)S(1)}, f32[4,16,10,1]{3,2,1,0:T(8,128)S(1)}, u32[]{:S(2)}, u32[]{:S(2)}) %collective-permute-start.3) | collective-permute-done | bytes 2592 | tf_op jit(solution)/shard_map/ppermute | solution.py:34
  112.3 1.7 %collective-permute-done.2 = f32[4,16,10,1]{3,2,1,0:T(8,128)S(1)} collective-permute-done((f32[4,16,10,1]{3,2,1,0:T(8,128)S(1)}, f32[4,16,10,1]{3,2,1,0:T(8,128)S(1)}, u32[]{:S(2)}, u32[]{:S(2)}) %collective-permute-start.2) | collective-permute-done | bytes 2592 | tf_op jit(solution)/shard_map/ppermute | solution.py:35
  114.6 0.5 fusion.90
  115.1 0.7 add.160
  (88 shorter events, 9.3 us)
Async XLA Ops:
  1.7 91.9 %collective-permute-start = (f32[4,16,1,128]{3,2,1,0:T(1,128)S(1)}, f32[4,16,1,128]{3,2,1,0:T(1,128)S(1)}, u32[]{:S(2)}, u32[]{:S(2)}) collective-permute-start(f32[4,16,1,128]{3,2,1,0:T(1,128)S(1)} %get-tuple-element.38), channel_id=1, source_target_pairs={{16,0},{32,16},{48,32},{64,48},{80,64},{96,80},{112,96},{17,1},{33... | collective-permute-start | bytes 98312 | tf_op jit(solution)/shard_map/ppermute | solution.py:35
  3.0 3.8 %copy-start.4 = (s32[1,9,128]{2,0,1:T(1,128)S(1)}, s32[1,9,128]{2,0,1:T(1,128)}, u32[]{:S(2)}) copy-start(s32[1,9,128]{2,0,1:T(1,128)} %param.21) | copy-start | bytes 13828
  3.0 90.6 %collective-permute-start.1 = (f32[4,16,1,128]{3,2,1,0:T(1,128)S(1)}, f32[4,16,1,128]{3,2,1,0:T(1,128)S(1)}, u32[]{:S(2)}, u32[]{:S(2)}) collective-permute-start(f32[4,16,1,128]{3,2,1,0:T(1,128)S(1)} %get-tuple-element.37), channel_id=1, source_target_pairs={{0,16},{16,32},{32,48},{48,64},{64,80},{80,96},{96,112},{1,17},{17... | collective-permute-start | bytes 98312 | tf_op jit(solution)/shard_map/ppermute | solution.py:34
  9.3 6.2 %copy-start = (f32[4,16,8,128]{3,2,1,0:T(8,128)S(1)}, f32[4,16,8,128]{3,2,1,0:T(8,128)}, u32[]{:S(2)}) copy-start(f32[4,16,8,128]{3,2,1,0:T(8,128)} %param.13) | copy-start | bytes 786436
  10.6 13.4 %collective-permute-start.5 = (f32[4,1,3,128]{3,0,2,1:T(4,128)S(1)}, f32[4,1,3,128]{3,0,2,1:T(4,128)S(1)}, u32[]{:S(2)}, u32[]{:S(2)}) collective-permute-start(f32[4,1,3,128]{3,0,2,1:T(4,128)S(1)} %get-tuple-element.46), channel_id=1, source_target_pairs={{16,0},{32,16},{48,32},{64,48},{80,64},{96,80},{112,96},{17,1},{33... | collective-permute-start | bytes 18440 | tf_op jit(solution)/shard_map/ppermute | solution.py:35
  11.9 3.7 %copy-start.5 = (f32[1,9,128]{2,0,1:T(1,128)S(1)}, f32[1,9,128]{2,0,1:T(1,128)}, u32[]{:S(2)}) copy-start(f32[1,9,128]{2,0,1:T(1,128)} %param.20) | copy-start | bytes 13828
  11.9 12.0 %collective-permute-start.4 = (f32[4,1,3,128]{3,0,2,1:T(4,128)S(1)}, f32[4,1,3,128]{3,0,2,1:T(4,128)S(1)}, u32[]{:S(2)}, u32[]{:S(2)}) collective-permute-start(f32[4,1,3,128]{3,0,2,1:T(4,128)S(1)} %get-tuple-element.45), channel_id=1, source_target_pairs={{0,16},{16,32},{32,48},{48,64},{64,80},{80,96},{96,112},{1,17},{17... | collective-permute-start | bytes 18440 | tf_op jit(solution)/shard_map/ppermute | solution.py:34
  15.6 0.7 copy-start.7
  15.6 0.7 copy-start.2
  16.3 0.7 copy-start.1
  16.3 0.7 copy-start.6
  17.7 0.7 copy-start.8
  23.2 0.7 copy-start.3
  24.0 24.6 %collective-permute-start.7 = (f32[4,5,1,128]{3,0,2,1:T(4,128)S(1)}, f32[4,5,1,128]{3,0,2,1:T(4,128)S(1)}, u32[]{:S(2)}, u32[]{:S(2)}) collective-permute-start(f32[4,5,1,128]{3,0,2,1:T(4,128)S(1)} %get-tuple-element.42), channel_id=1, source_target_pairs={{1,0},{2,1},{3,2},{4,3},{5,4},{6,5},{7,6},{8,7},{9,8},{10,9},{11,1... | collective-permute-start | bytes 30728 | tf_op jit(solution)/shard_map/ppermute | solution.py:35
  30.1 18.5 %collective-permute-start.6 = (f32[4,5,1,128]{3,0,2,1:T(4,128)S(1)}, f32[4,5,1,128]{3,0,2,1:T(4,128)S(1)}, u32[]{:S(2)}, u32[]{:S(2)}) collective-permute-start(f32[4,5,1,128]{3,0,2,1:T(4,128)S(1)} %get-tuple-element.41), channel_id=1, source_target_pairs={{0,1},{1,2},{2,3},{3,4},{4,5},{5,6},{6,7},{7,8},{8,9},{9,10},{10,1... | collective-permute-start | bytes 30728 | tf_op jit(solution)/shard_map/ppermute | solution.py:34
  79.8 5.9 %collective-permute-start.9 = (f32[4,1,3,128]{3,0,2,1:T(4,128)S(1)}, f32[4,1,3,128]{3,0,2,1:T(4,128)S(1)}, u32[]{:S(2)}, u32[]{:S(2)}) collective-permute-start(f32[4,1,3,128]{3,0,2,1:T(4,128)S(1)} %get-tuple-element.44), channel_id=1, source_target_pairs={{16,0},{32,16},{48,32},{64,48},{80,64},{96,80},{112,96},{17,1},{33... | collective-permute-start | bytes 18440 | tf_op jit(solution)/shard_map/ppermute | solution.py:35
  81.1 4.8 %collective-permute-start.8 = (f32[4,1,3,128]{3,0,2,1:T(4,128)S(1)}, f32[4,1,3,128]{3,0,2,1:T(4,128)S(1)}, u32[]{:S(2)}, u32[]{:S(2)}) collective-permute-start(f32[4,1,3,128]{3,0,2,1:T(4,128)S(1)} %get-tuple-element.43), channel_id=1, source_target_pairs={{0,16},{16,32},{32,48},{48,64},{64,80},{80,96},{96,112},{1,17},{17... | collective-permute-start | bytes 18440 | tf_op jit(solution)/shard_map/ppermute | solution.py:34
  85.9 16.0 %collective-permute-start.11 = (f32[4,5,1,128]{3,0,2,1:T(4,128)S(1)}, f32[4,5,1,128]{3,0,2,1:T(4,128)S(1)}, u32[]{:S(2)}, u32[]{:S(2)}) collective-permute-start(f32[4,5,1,128]{3,0,2,1:T(4,128)S(1)} %get-tuple-element.40), channel_id=1, source_target_pairs={{1,0},{2,1},{3,2},{4,3},{5,4},{6,5},{7,6},{8,7},{9,8},{10,9},{11,1... | collective-permute-start | bytes 30728 | tf_op jit(solution)/shard_map/ppermute | solution.py:35
  91.7 10.2 %collective-permute-start.10 = (f32[4,5,1,128]{3,0,2,1:T(4,128)S(1)}, f32[4,5,1,128]{3,0,2,1:T(4,128)S(1)}, u32[]{:S(2)}, u32[]{:S(2)}) collective-permute-start(f32[4,5,1,128]{3,0,2,1:T(4,128)S(1)} %get-tuple-element.39), channel_id=1, source_target_pairs={{0,1},{1,2},{2,3},{3,4},{4,5},{5,6},{6,7},{7,8},{8,9},{9,10},{10,1... | collective-permute-start | bytes 30728 | tf_op jit(solution)/shard_map/ppermute | solution.py:34
  93.9 18.4 %collective-permute-start.3 = (f32[4,16,10,1]{3,2,1,0:T(8,128)S(1)}, f32[4,16,10,1]{3,2,1,0:T(8,128)S(1)}, u32[]{:S(2)}, u32[]{:S(2)}) collective-permute-start(f32[4,16,10,1]{3,2,1,0:T(8,128)S(1)} %get-tuple-element.31), channel_id=1, source_target_pairs={{0,1},{1,2},{2,3},{3,4},{4,5},{5,6},{6,7},{7,8},{8,9},{9,10},{10,1... | collective-permute-start | bytes 7688 | tf_op jit(solution)/shard_map/ppermute | solution.py:34
  95.9 18.2 %collective-permute-start.2 = (f32[4,16,10,1]{3,2,1,0:T(8,128)S(1)}, f32[4,16,10,1]{3,2,1,0:T(8,128)S(1)}, u32[]{:S(2)}, u32[]{:S(2)}) collective-permute-start(f32[4,16,10,1]{3,2,1,0:T(8,128)S(1)} %get-tuple-element.30), channel_id=1, source_target_pairs={{1,0},{2,1},{3,2},{4,3},{5,4},{6,5},{7,6},{8,7},{9,8},{10,9},{11,1... | collective-permute-start | bytes 7688 | tf_op jit(solution)/shard_map/ppermute | solution.py:35
where the time goes:
time: 117 us; the launch traced here: 116 us
  starting transfers between devices  38.2 us (33%)
  matrix products  31.9 us (27%)
  other arithmetic  20.6 us (18%)
  local copies, waits for them, and re-layouts  14.6 us (12%)
  waiting for transfers between devices  9.23 us (8%)
  between operations  1.3 us (1%)
    ppermute x6, starting transfers between devices, with_halo(): after = lax.ppermute(leading, axis, down)  21.8 us
    dot_general x14, matrix products, pick_rows(): jnp.einsum('tpf,ctf->ctp', table, field, precision=EXACT, preferred_eleme...  17.4 us
    ppermute x6, starting transfers between devices, with_halo(): before = lax.ppermute(last, axis, up)  16.4 us
    scatter-add x1, other arithmetic, floe_side(): jnp.zeros((floe_count,), jnp.float32).at[floe_index].add(weight)  9.18 us
    scatter-add x1, other arithmetic, floe_side(): jnp.zeros((2, floe_count), jnp.float32).at[:, floe_index]  8.4 us
    dot_general x8, matrix products, spread_rows(): jnp.einsum('tpf,ctp->ctf', table, values, precision=EXACT, preferred_elem...  7.63 us
    ppermute x6, waiting for transfers between devices, with_halo(): before = lax.ppermute(last, axis, up)  7.47 us
    gather x2, local copies, waits for them, and re-layouts, floe_side(): salt_flux = SALT_COEF * weight * floe_props[1][floe_index]  7.3 us
  transfers between devices with their start and end apart: 12, of which 3 were waited for; matrix products, arithmetic and copies ran while one was open for 54% of the time, Pallas kernels for 0%

commit v1 on v0

v1 whole, which is shorter than its diff:
```python
import jax
import jax.numpy as jnp
from jax import lax
from jax.experimental import pallas as pl
from jax.experimental.pallas import tpu as pltpu
from jax.sharding import PartitionSpec as P

F32 = jnp.float32
BF16 = jnp.bfloat16
I32 = jnp.int32

TILE = 128
TILES = 4
SUBSTEPS = 4
LEV = 16
BUCKETS = 9
ENTRIES = BUCKETS * 128
TIME_STEP = 0.05
CONTACT_STIFF = 2.0
CONTACT_DAMP = 0.2
BOND_DAMP = 0.3
DRAG_COEF = 0.5
HEAT_COEF = 0.3
SALT_COEF = 0.2
FREEZE = -1.8
DIFFUSE_SIDE = 0.15
DIFFUSE_DEPTH = 0.2
CORIOLIS = 0.3
PRESSURE_COEF = 0.1
THERMAL_EXP = 0.2
HALINE_CONTR = 0.8
AXES = ("ocx", "ocy")
VMEM_SPEC = pl.BlockSpec(memory_space=pltpu.VMEM)


def call(kernel, outs, *args, cost=0):
    return pl.pallas_call(
        kernel,
        out_shape=outs,
        in_specs=[VMEM_SPEC] * len(args),
        out_specs=jax.tree.map(lambda _: VMEM_SPEC, outs),
        cost_estimate=pl.CostEstimate(flops=cost, bytes_accessed=1 << 16, transcendentals=0),
    )(*args)


def shaped(*shape, dtype=F32):
    return jax.ShapeDtypeStruct(shape, dtype)


def split3(x):
    hi = x.astype(BF16).astype(F32)
    rest = x - hi
    mid = rest.astype(BF16).astype(F32)
    return jnp.concatenate([hi, mid, rest - mid], axis=0).astype(BF16)


def join3(y):
    n = y.shape[0] // 3
    return y[:n] + y[n : 2 * n] + y[2 * n :]


def dot_nn(a, b):
    return lax.dot_general(a, b, (((1,), (0,)), ((), ())), preferred_element_type=F32)


def dot_nt(a, b):
    return lax.dot_general(a, b, (((1,), (1,)), ((), ())), preferred_element_type=F32)


def lanes_row(ref):
    return jnp.concatenate([ref[m] for m in range(BUCKETS)], axis=1)


def one_hot(row):
    n = row.shape[1]
    ids = lax.broadcasted_iota(I32, (128, n), 0)
    return jnp.where(ids == jnp.broadcast_to(row, (128, n)), 1.0, 0.0).astype(BF16)


def is_even(axis):
    return lax.rem(lax.axis_index(axis), 2) == 0


def send_both(even, toward_plus, toward_minus, even_ref, odd_ref, row, rows):
    even_ref[pl.ds(row, rows), :] = jnp.where(even, toward_plus, toward_minus)
    odd_ref[pl.ds(row, rows), :] = jnp.where(even, toward_minus, toward_plus)


def bucket_rows(fields, a):
    rows = [f[:, (3 * a + b) * 128 : (3 * a + b + 1) * 128] for f in fields for b in range(3)]
    return jnp.concatenate(rows, axis=0)


def sample_kernel(ocean_ref, cell_ref, even_ref, odd_ref, own_ref):
    even = is_even("ocx")
    cells = lanes_row(cell_ref)
    table = one_hot(cells & 127)
    surface = jnp.concatenate([ocean_ref[pl.ds(f * 128, 8), :] for f in range(3)], axis=0)
    picked = join3(dot_nn(split3(surface), table))
    row_hit = lax.broadcasted_iota(I32, (8, ENTRIES), 0) == jnp.broadcast_to(
        cells >> 7, (8, ENTRIES)
    )
    fields = [
        jnp.sum(jnp.where(row_hit, picked[8 * f : 8 * f + 8], 0.0), axis=0, keepdims=True)
        for f in range(3)
    ]
    send_both(even, bucket_rows(fields, 2), bucket_rows(fields, 0), even_ref, odd_ref, 0, 9)
    own_ref[pl.ds(0, 9), :] = bucket_rows(fields, 1)
    first = ocean_ref[pl.ds(0, 64, stride=8), :]
    last = ocean_ref[pl.ds(7, 64, stride=8), :]
    send_both(even, last, first, even_ref, odd_ref, 16, 64)


def column_kernel(ocean_ref, floe_ref, weight_ref, props_ref, cols_ref, table_ref, area_ref, salt_ref):
    for f in range(4):
        turned = ocean_ref[pl.ds(f * 128, 128), :].T
        cols_ref[pl.ds(f, 1), :] = turned[127:128]
        cols_ref[pl.ds(4 + f, 1), :] = turned[0:1]
    floes = lanes_row(floe_ref)
    weight = lanes_row(weight_ref)
    table = one_hot(floes & 127)
    table_ref[...] = table
    tile_hit = (lax.broadcasted_iota(I32, (8, ENTRIES), 0) & 3) == jnp.broadcast_to(
        floes >> 7, (8, ENTRIES)
    )
    spread = jnp.where(tile_hit, jnp.broadcast_to(weight, (8, ENTRIES)), 0.0)
    area_ref[...] = join3(dot_nt(split3(spread), table))
    thick = jnp.concatenate(
        [props_ref[pl.ds(1, 1), pl.ds(t * 128, 128)] for t in range(TILES)] * 2, axis=0
    )
    picked = join3(dot_nn(split3(thick), table))
    chosen = jnp.sum(jnp.where(tile_hit, picked, 0.0)[:4], axis=0, keepdims=True)
    salt_ref[...] = SALT_COEF * weight * chosen


def tile_rows(ref, k):
    return jnp.concatenate(
        [ref[pl.ds(k, 1), pl.ds(t * 128, 128)] for t in range(TILES)], axis=0
    )


def pair_forces(x8, v8, reach_ref, contact_ref, bond_ref):
    turned = jnp.concatenate([x8, v8], axis=0).T
    rows = [[None] * TILES for _ in range(2)]
    step = 32

    def column(c, lo):
        return jnp.broadcast_to(turned[lo : lo + step, c : c + 1], (step, 128))

    def wide(row):
        return jnp.broadcast_to(row, (step, 128))

    for t in range(TILES):
        total_x = jnp.zeros((8, 128), F32)
        total_y = jnp.zeros((8, 128), F32)
        for lo in range(0, 128, step):
            part = pl.ds(lo, step)
            dx = column(t, lo) - wide(x8[t : t + 1])
            dy = column(4 + t, lo) - wide(x8[4 + t : 5 + t])
            depth = jnp.maximum(1.0 - (dx * dx + dy * dy) * reach_ref[t, part, :], 0.0)
            stiff = depth * contact_ref[t, part, :]
            damp = (CONTACT_DAMP / CONTACT_STIFF) * stiff + bond_ref[t, part, :]
            dvx = column(8 + t, lo) - wide(v8[t : t + 1])
            dvy = column(12 + t, lo) - wide(v8[4 + t : 5 + t])
            fx = damp * dvx - stiff * dx
            fy = damp * dvy - stiff * dy
            total_x = total_x + jnp.sum(fx.reshape(step // 8, 8, 128), axis=0)
            total_y = total_y + jnp.sum(fy.reshape(step // 8, 8, 128), axis=0)
        rows[0][t] = jnp.sum(total_x, axis=0, keepdims=True)
        rows[1][t] = jnp.sum(total_y, axis=0, keepdims=True)
    return jnp.concatenate(rows[0] + rows[1], axis=0)


def state_rows(state_ref):
    x8 = jnp.concatenate([tile_rows(state_ref, 0), tile_rows(state_ref, 1)], axis=0)
    v8 = jnp.concatenate([tile_rows(state_ref, 2), tile_rows(state_ref, 3)], axis=0)
    return x8, v8


def pair_kernel(
    pairs_ref, bonds_ref, broken_ref, props_ref, state_ref, reach_ref, contact_ref, bond_ref, force_ref
):
    def differences(ref, t, n):
        ids = lax.broadcasted_iota(I32, (128, n), 0)
        first = jnp.broadcast_to(ref[0, pl.ds(t, 1), :], (128, n))
        second = jnp.broadcast_to(ref[1, pl.ds(t, 1), :], (128, n))
        return jnp.where(ids == second, 1.0, 0.0) - jnp.where(ids == first, 1.0, 0.0)

    radius = tile_rows(props_ref, 0)
    radius_columns = jnp.concatenate([radius, radius], axis=0).T
    for t in range(TILES):
        slots = differences(pairs_ref, t, 512).astype(BF16)
        contact_ref[t] = -CONTACT_STIFF * dot_nt(slots, slots)
        alive = jnp.broadcast_to(broken_ref[pl.ds(t, 1), :], (128, 256)) == 0
        ends = jnp.where(alive, differences(bonds_ref, t, 256), 0.0).astype(BF16)
        bond_ref[t] = -BOND_DAMP * dot_nt(ends, ends)
        reach = jnp.broadcast_to(radius_columns[:, t : t + 1], (128, 128)) + jnp.broadcast_to(
            radius[t : t + 1], (128, 128)
        )
        reach_ref[t] = 1.0 / (reach * reach)
    x8, v8 = state_rows(state_ref)
    force_ref[...] = pair_forces(x8, v8, reach_ref, contact_ref, bond_ref)


def from_sides(even, got_even, got_odd):
    return jnp.where(even, got_odd, got_even), jnp.where(even, got_even, got_odd)


def turn_rows(low, own, high, count):
    return [
        jnp.concatenate(
            [src[3 * f + b : 3 * f + b + 1] for f in range(count) for src in (low, own, high)],
            axis=0,
        )
        for b in range(3)
    ]


def turn_kernel(count, with_cols):
    def kernel(*refs):
        if with_cols:
            got_even_ref, got_odd_ref, own_ref, cols_ref, even_ref, odd_ref, keep_ref = refs
        else:
            got_even_ref, got_odd_ref, own_ref, even_ref, odd_ref, keep_ref = refs
        part = pl.ds(0, 3 * count)
        low, high = from_sides(is_even("ocx"), got_even_ref[part, :], got_odd_ref[part, :])
        down, keep, up = turn_rows(low, own_ref[part, :], high, count)
        even = is_even("ocy")
        send_both(even, up, down, even_ref, odd_ref, 0, 3 * count)
        if with_cols:
            send_both(even, cols_ref[0:4], cols_ref[4:8], even_ref, odd_ref, 12, 4)
        keep_ref[part, :] = keep

    return kernel


def entry_rows(got_even_ref, got_odd_ref, keep_ref, count):
    part = pl.ds(0, 3 * count)
    low, high = from_sides(is_even("ocy"), got_even_ref[part, :], got_odd_ref[part, :])
    keep = keep_ref[part, :]
    return [
        jnp.concatenate(
            [src[3 * f + a : 3 * f + a + 1] for a in range(3) for src in (low, keep, high)], axis=1
        )
        for f in range(count)
    ]


def floe_kernel(
    got_even_ref,
    got_odd_ref,
    keep_ref,
    floe_ref,
    weight_ref,
    table_ref,
    area_ref,
    salt_ref,
    reach_ref,
    contact_ref,
    bond_ref,
    force_ref,
    state_ref,
    props_ref,
    next_ref,
    even_ref,
    odd_ref,
    own_ref,
):
    samples = entry_rows(got_even_ref, got_odd_ref, keep_ref, 3)
    weight = lanes_row(weight_ref)
    floes = lanes_row(floe_ref)
    table = table_ref[...]
    ids = lax.broadcasted_iota(I32, (8, ENTRIES), 0)
    tile_hit = (ids & 3) == jnp.broadcast_to(floes >> 7, (8, ENTRIES))
    wide = jnp.where(
        ids < 4,
        jnp.broadcast_to(weight * samples[0], (8, ENTRIES)),
        jnp.broadcast_to(weight * samples[1], (8, ENTRIES)),
    )
    drag = join3(dot_nt(split3(jnp.where(tile_hit, wide, 0.0)), table))
    area = area_ref[...]
    radius = tile_rows(props_ref, 0)
    inv_mass = 1.0 / (tile_rows(props_ref, 1) * radius * radius)
    push = TIME_STEP * jnp.concatenate([inv_mass, inv_mass], axis=0)
    x8, v8 = state_rows(state_ref)
    mean = jnp.zeros((8, 128), F32)
    for substep in range(SUBSTEPS):
        if substep == 0:
            force = force_ref[...]
        else:
            force = pair_forces(x8, v8, reach_ref, contact_ref, bond_ref)
        force = force + DRAG_COEF * (drag - area * v8)
        v8 = v8 + push * force
        x8 = x8 + TIME_STEP * v8
        mean = mean + v8 * (1.0 / SUBSTEPS)
    for k in range(2):
        for t in range(TILES):
            lanes = pl.ds(t * 128, 128)
            next_ref[pl.ds(k, 1), lanes] = x8[4 * k + t : 4 * k + t + 1]
            next_ref[pl.ds(2 + k, 1), lanes] = v8[4 * k + t : 4 * k + t + 1]
    picked = jnp.where(tile_hit, join3(dot_nn(split3(mean), table)), 0.0)
    flux = [
        DRAG_COEF
        * weight
        * (jnp.sum(picked[4 * k : 4 * k + 4], axis=0, keepdims=True) - samples[k])
        for k in range(2)
    ]
    flux = flux + [HEAT_COEF * weight * (FREEZE - samples[2]), salt_ref[...]]
    send_both(
        is_even("ocx"), bucket_rows(flux, 2), bucket_rows(flux, 0), even_ref, odd_ref, 0, 12
    )
    own_ref[pl.ds(0, 12), :] = bucket_rows(flux, 1)


def ocean_kernel(ocean_ref, x_even_ref, x_odd_ref, y_even_ref, y_odd_ref, out_ref, low_ref, high_ref):
    i, j = lax.axis_index("ocx"), lax.axis_index("ocy")
    x_even, y_even = lax.rem(i, 2) == 0, lax.rem(j, 2) == 0
    rows = pl.ds(16, 64)
    low, high = from_sides(x_even, x_even_ref[rows, :], x_odd_ref[rows, :])
    low_ref[...] = jnp.where(i == 0, 0.0, low)
    high_ref[...] = jnp.where(i == lax.axis_size("ocx") - 1, 0.0, high)
    rows = pl.ds(12, 4)
    left, right = from_sides(y_even, y_even_ref[rows, :], y_odd_ref[rows, :])
    left = jnp.where(j == 0, 0.0, left)
    right = jnp.where(j == lax.axis_size("ocy") - 1, 0.0, right)
    turned = jnp.concatenate([left, right], axis=0).T
    sub = lax.broadcasted_iota(I32, (8, 128), 0)
    lane = lax.broadcasted_iota(I32, (8, 128), 1)
    at_low, at_high = sub == 0, sub == 7
    at_left, at_right = lane == 0, lane == 127

    def block(f, l):
        return ocean_ref[pl.ds((f * LEV + l) * 8, 8), :]

    def neighbours(f, l, here):
        k = f * LEV + l
        below = jnp.where(
            at_low, jnp.broadcast_to(low_ref[pl.ds(k, 1), :], (8, 128)), pltpu.roll(here, 1, 0)
        )
        above = jnp.where(
            at_high, jnp.broadcast_to(high_ref[pl.ds(k, 1), :], (8, 128)), pltpu.roll(here, 7, 0)
        )
        edge = turned[l * 8 : l * 8 + 8]
        left = jnp.where(
            at_left, jnp.broadcast_to(edge[:, f : f + 1], (8, 128)), pltpu.roll(here, 1, 1)
        )
        right = jnp.where(
            at_right, jnp.broadcast_to(edge[:, 4 + f : 5 + f], (8, 128)), pltpu.roll(here, 127, 1)
        )
        return below, above, left, right

    grad_x = jnp.zeros((8, 128), F32)
    grad_y = jnp.zeros((8, 128), F32)
    for l in range(LEV):
        here = [block(f, l) for f in range(4)]
        around = [neighbours(f, l, here[f]) for f in range(4)]
        below, above, left, right = zip(*around)
        grad_x = grad_x + (
            (0.5 * HALINE_CONTR) * (above[3] - below[3]) - (0.5 * THERMAL_EXP) * (above[2] - below[2])
        )
        grad_y = grad_y + (
            (0.5 * HALINE_CONTR) * (right[3] - left[3]) - (0.5 * THERMAL_EXP) * (right[2] - left[2])
        )
        for f in range(4):
            side = below[f] + above[f] + left[f] + right[f] - 4.0 * here[f]
            depth = block(f, max(l - 1, 0)) + block(f, min(l + 1, LEV - 1)) - 2.0 * here[f]
            new = here[f] + DIFFUSE_SIDE * side + DIFFUSE_DEPTH * depth
            if f == 0:
                new = new + CORIOLIS * here[1] - PRESSURE_COEF * grad_x
            if f == 1:
                new = new - CORIOLIS * here[0] - PRESSURE_COEF * grad_y
            out_ref[pl.ds((f * LEV + l) * 8, 8), :] = new


def forcing_kernel(got_even_ref, got_odd_ref, keep_ref, cell_ref, ocean_ref, out_ref):
    cells = lanes_row(cell_ref)
    table = one_hot(cells & 127)
    row_hit = lax.broadcasted_iota(I32, (8, ENTRIES), 0) == jnp.broadcast_to(
        cells >> 7, (8, ENTRIES)
    )
    flux = entry_rows(got_even_ref, got_odd_ref, keep_ref, 4)
    spread = jnp.concatenate(
        [jnp.where(row_hit, jnp.broadcast_to(row, (8, ENTRIES)), 0.0) for row in flux], axis=0
    )
    forcing = join3(dot_nt(split3(spread), table))
    out_ref[...] = ocean_ref[...]
    for f in range(4):
        rows = pl.ds(f * LEV * 8, 8)
        out_ref[rows, :] = ocean_ref[rows, :] + forcing[8 * f : 8 * f + 8]


def pairings(nx, ny):
    def both(pair_of):
        return [(i * ny + j, pair_of(i, j)) for i in range(nx) for j in range(ny)]

    def odd_x(i, j):
        if i in (0, nx - 1):
            return i * ny + (j ^ 1)
        return (i + 1 if i % 2 else i - 1) * ny + j

    def odd_y(i, j):
        if j in (0, ny - 1):
            return (i ^ 1) * ny + j
        return i * ny + (j + 1 if j % 2 else j - 1)

    return (
        both(lambda i, j: (i ^ 1) * ny + j),
        both(odd_x),
        both(lambda i, j: i * ny + (j ^ 1)),
        both(odd_y),
    )


def shards(nx, ny):
    x_even, x_odd, y_even, y_odd = pairings(nx, ny)

    def body(
        ocean_state,
        floe_state,
        floe_props,
        contact_pairs,
        bond_ends,
        bond_broken,
        couple_floe,
        couple_weight,
        couple_cell,
    ):
        ocean = ocean_state.reshape(4 * LEV * 8, 128)
        floe = couple_floe.reshape(BUCKETS, 1, 128)
        weight = couple_weight.reshape(BUCKETS, 1, 128)
        cell = couple_cell.reshape(BUCKETS, 1, 128)
        small = shaped(16, 128)
        send_even, send_odd, own = call(
            sample_kernel, (shaped(80, 128), shaped(80, 128), small), ocean, cell
        )
        ge_x = lax.ppermute(send_even, AXES, x_even)
        go_x = lax.ppermute(send_odd, AXES, x_odd)
        cols, table, area, salt = call(
            column_kernel,
            (shaped(8, 128), shaped(128, ENTRIES, dtype=BF16), shaped(8, 128), shaped(1, ENTRIES)),
            ocean,
            floe,
            weight,
            floe_props,
        )
        send_even, send_odd, keep = call(
            turn_kernel(3, True), (small, small, small), ge_x, go_x, own, cols
        )
        ge_y = lax.ppermute(send_even, AXES, y_even)
        go_y = lax.ppermute(send_odd, AXES, y_odd)
        square = shaped(TILES, 128, 128)
        reach, contact, bond, force = call(
            pair_kernel,
            (square, square, square, shaped(8, 128)),
            contact_pairs,
            bond_ends,
            bond_broken,
            floe_props,
            floe_state,
        )
        floe_next, send_even, send_odd, own = call(
            floe_kernel,
            (shaped(4, 512), small, small, small),
            ge_y,
            go_y,
            keep,
            floe,
            weight,
            table,
            area,
            salt,
            reach,
            contact,
            bond,
            force,
            floe_state,
            floe_props,
        )
        he_x = lax.ppermute(send_even, AXES, x_even)
        ho_x = lax.ppermute(send_odd, AXES, x_odd)
        send_even, send_odd, keep = call(
            turn_kernel(4, False), (small, small, small), he_x, ho_x, own
        )
        he_y = lax.ppermute(send_even, AXES, y_even)
        ho_y = lax.ppermute(send_odd, AXES, y_odd)
        moved = pl.pallas_call(
            ocean_kernel,
            out_shape=shaped(4 * LEV * 8, 128),
            in_specs=[VMEM_SPEC] * 5,
            out_specs=VMEM_SPEC,
            scratch_shapes=[pltpu.VMEM((64, 128), F32), pltpu.VMEM((64, 128), F32)],
        )(ocean, ge_x, go_x, ge_y, go_y)
        ocean_next = call(forcing_kernel, shaped(4 * LEV * 8, 128), he_y, ho_y, keep, cell, moved)
        return (ocean_next.reshape(ocean_state.shape), floe_next)

    return body


def solution(mesh):
    in_specs = (
        P(None, None, "ocx", "ocy"),
        P(None, ("ocx", "ocy")),
        P(None, ("ocx", "ocy")),
        P(None, ("ocx", "ocy"), None),
        P(None, ("ocx", "ocy"), None),
        P(("ocx", "ocy"), None),
        P(("ocx", "ocy"), None, None),
        P(("ocx", "ocy"), None, None),
        P(("ocx", "ocy"), None, None),
    )
    out_specs = (P(None, None, "ocx", "ocy"), P(None, ("ocx", "ocy")))
    body = shards(mesh.shape["ocx"], mesh.shape["ocy"])
    return jax.shard_map(body, mesh=mesh, in_specs=in_specs, out_specs=out_specs, check_vma=False)
```

time: 117 us -> 36 us (0.31)
  matrix products: 31.9 us -> 0 us
  starting transfers between devices: 38.2 us -> 9.34 us
  other arithmetic: 20.6 us -> 0 us
  Pallas kernels: 0 us -> 16.9 us
  local copies, waits for them, and re-layouts: 14.6 us -> 2.39 us
  waiting for transfers between devices: 9.23 us -> 6.34 us
    dot_general x40 -> x0, matrix products: 31.9 us -> none  [the longest x14 17.4 us: pick_rows(): jnp.einsum('tpf,ctf->ctp', table, field, precision=EXACT, preferred_eleme...]
    ppermute x12 -> x8, starting transfers between devices: 38.2 us -> 9.34 us  [the longest x1 2.7 us: body(): go_y = lax.ppermute(send_odd, AXES, y_odd)]
    scatter-add x4 -> x0, other arithmetic: 17.6 us -> none  [the longest x1 9.18 us: floe_side(): jnp.zeros((floe_count,), jnp.float32).at[floe_index].add(weight)]
    pallas_call x0 -> x8, Pallas kernels: none -> 16.9 us  [the longest x7 14.7 us: call(): pl.pallas_call(kernel, out_shape=outs, in_specs=[VMEM_SPEC] * len(args),...]
    gather x4 -> x0, local copies, waits for them, and re-layouts: 9.95 us -> none  [the longest x2 7.3 us: floe_side(): salt_flux = SALT_COEF * weight * floe_props[1][floe_index]]
    ppermute x12 -> x8, waiting for transfers between devices: 9.23 us -> 6.34 us  [the longest x1 2.56 us: body(): ho_x = lax.ppermute(send_odd, AXES, x_odd)]
    slice x9 -> x0, local copies, waits for them, and re-layouts: 1.59 us -> none  [the longest x2 1.08 us: with_halo(): last = lax.slice_in_dim(array, length - width, length, axis=dim)]
    add x3 -> x0, other arithmetic: 1.22 us -> none  [the longest x1 0.74 us: ocean_update(): return interior + tendency]
  transfers between devices with their start and end apart: 12 -> 8, of which waited for: 3 -> 5; matrix products, arithmetic and copies ran while one was open for 54% -> 0% of each run, Pallas kernels for 0% -> 18%
where the time goes in v1:
time: 36 us; the launch traced here: 35.6 us
  Pallas kernels  16.9 us (47%)
  starting transfers between devices  9.34 us (26%)
  waiting for transfers between devices  6.34 us (18%)
  local copies, waits for them, and re-layouts  2.39 us (7%)
  between operations  0.67 us (2%)
    pallas_call x7, Pallas kernels, call(): pl.pallas_call(kernel, out_shape=outs, in_specs=[VMEM_SPEC] * len(args),...  14.7 us
    ppermute x1, starting transfers between devices, body(): go_y = lax.ppermute(send_odd, AXES, y_odd)  2.7 us
    ppermute x1, starting transfers between devices, body(): ho_y = lax.ppermute(send_odd, AXES, y_odd)  2.7 us
    ppermute x1, waiting for transfers between devices, body(): ho_x = lax.ppermute(send_odd, AXES, x_odd)  2.56 us
    unnamed x16, local copies, waits for them, and re-layouts  2.39 us
    pallas_call x1, Pallas kernels, body(): pl.pallas_call(ocean_kernel, out_shape=shaped(4 * LEV * 8, 128), in_specs...  2.18 us
    ppermute x1, starting transfers between devices, body(): go_x = lax.ppermute(send_odd, AXES, x_odd)  1.92 us
    ppermute x1, starting transfers between devices, body(): ge_y = lax.ppermute(send_even, AXES, y_even)  1.92 us
  transfers between devices with their start and end apart: 8, of which 5 were waited for; matrix products, arithmetic and copies ran while one was open for 0% of the time, Pallas kernels for 18%

profile of v1, /device:TPU:24, one launch (start us, length us, event | category | flops | bytes accessed | tf_op | source)
XLA Modules:
  0.0 35.6 jit_solution(685718109159390865)
XLA Ops:
  0.6 1.8 %shard_map.104 = (f32[80,128]{1,0:T(8,128)}, f32[80,128]{1,0:T(8,128)}, f32[16,128]{1,0:T(8,128)}) custom-call(f32[512,128]{1,0:T(8,128)} %bitcast.5, s32[9,1,128]{2,1,0:T(1,128)} %bitcast.13), custom_call_target="tpu_custom_call" | custom-call | bytes 65536 | tf_op jit(solution)/shard_map/pallas_call | solution.py:37
  2.4 0.0 collective-permute-start
  2.4 1.9 %collective-permute-start.1 = (f32[80,128]{1,0:T(8,128)}, f32[80,128]{1,0:T(8,128)S(1)}, u32[]{:S(2)}, u32[]{:S(2)}) collective-permute-start(f32[80,128]{1,0:T(8,128)} %get-tuple-element.24), channel_id=1, source_target_pairs={{0,1},{1,0},{2,3},{3,2},{4,5},{5,4},{6,7},{7,6},{8,9},{9,8},{10,11... | collective-permute-start | bytes 122888 | tf_op jit(solution)/shard_map/ppermute | solution.py:437
  4.4 1.9 %shard_map.105 = (f32[8,128]{1,0:T(8,128)}, bf16[128,1152]{1,0:T(8,128)(2,1)}, f32[8,128]{1,0:T(8,128)}, f32[1,1152]{1,0:T(1,128)}) custom-call(f32[512,128]{1,0:T(8,128)} %bitcast.6, s32[9,1,128]{2,1,0:T(1,128)} %bitcast.9, f32[9,1,128]{2,1,0:T(1,128)} %bitcast.11, f32[2,512]{1,0:T(2,128)} %props_ref.5), custom_call_target="tpu_custom_call" | custom-call | bytes 65536 | tf_op jit(solution)/shard_map/pallas_call | solution.py:37
  6.2 0.0 collective-permute-done.refs_0_.x_even_ref
  6.2 0.0 copy-start
  6.3 0.4 %collective-permute-done.1.refs_1_.x_odd_ref = f32[80,128]{1,0:T(8,128)S(1)} collective-permute-done((f32[80,128]{1,0:T(8,128)}, f32[80,128]{1,0:T(8,128)S(1)}, u32[]{:S(2)}, u32[]{:S(2)}) %collective-permute-start.1) | collective-permute-done | bytes 40992 | tf_op jit(solution)/shard_map/ppermute | solution.py:437
  6.6 0.0 copy-start.1
  6.7 0.2 copy-done
  6.9 0.4 %copy-done.1 = f32[80,128]{1,0:T(8,128)} copy-done((f32[80,128]{1,0:T(8,128)}, f32[80,128]{1,0:T(8,128)S(1)}, u32[]{:S(2)}) %copy-start.1) | copy-done | bytes 40984
  7.3 1.4 %shard_map.106 = (f32[16,128]{1,0:T(8,128)}, f32[16,128]{1,0:T(8,128)}, f32[16,128]{1,0:T(8,128)}) custom-call(f32[80,128]{1,0:T(8,128)} %copy-done, f32[80,128]{1,0:T(8,128)} %copy-done.1, f32[16,128]{1,0:T(8,128)} %get-tuple-element.25.refs_2_, f32[8,128]{1,0:T(8,128)} %get-tuple-element.26.refs_3_), custom_call_target="tpu_custom_call" | custom-call | bytes 65536 | tf_op jit(solution)/shard_map/pallas_call | solution.py:37
  8.7 1.9 %collective-permute-start.2 = (f32[16,128]{1,0:T(8,128)}, f32[16,128]{1,0:T(8,128)S(1)}, u32[]{:S(2)}, u32[]{:S(2)}) collective-permute-start(f32[16,128]{1,0:T(8,128)} %get-tuple-element.27), channel_id=1, source_target_pairs={{0,1},{1,0},{2,3},{3,2},{4,5},{5,4},{6,7},{7,6},{8,9},{9,8},{10,11... | collective-permute-start | bytes 24584 | tf_op jit(solution)/shard_map/ppermute | solution.py:449
  10.6 2.7 %collective-permute-start.3 = (f32[16,128]{1,0:T(8,128)}, f32[16,128]{1,0:T(8,128)S(1)}, u32[]{:S(2)}, u32[]{:S(2)}) collective-permute-start(f32[16,128]{1,0:T(8,128)} %get-tuple-element.28), channel_id=1, source_target_pairs={{0,16},{1,2},{2,1},{3,4},{4,3},{5,6},{6,5},{7,8},{8,7},{9,10},{10,... | collective-permute-start | bytes 24584 | tf_op jit(solution)/shard_map/ppermute | solution.py:450
  13.3 2.3 %shard_map.107 = (f32[4,128,128]{2,1,0:T(8,128)}, f32[4,128,128]{2,1,0:T(8,128)}, f32[4,128,128]{2,1,0:T(8,128)}, f32[8,128]{1,0:T(8,128)}) custom-call(s32[2,4,512]{2,1,0:T(4,128)} %pairs_ref.1, s32[2,4,256]{2,1,0:T(4,128)} %bonds_ref.1, s32[4,256]{1,0:T(4,128)} %broken_ref.1, f32[2,512]{1,0:T(2,128)} %props_ref.5, f32[4,512]{1,0:T(4,128)} %state_ref.3), custom_call_target="tpu_custom_call" | custom-call | bytes 65536 | tf_op jit(solution)/shard_map/pallas_call | solution.py:37
  15.6 0.0 collective-permute-done.2.got_even_ref.y_even_ref
  15.6 0.0 copy-start.2
  15.6 1.0 %collective-permute-done.3.got_odd_ref.y_odd_ref = f32[16,128]{1,0:T(8,128)S(1)} collective-permute-done((f32[16,128]{1,0:T(8,128)}, f32[16,128]{1,0:T(8,128)S(1)}, u32[]{:S(2)}, u32[]{:S(2)}) %collective-permute-start.3) | collective-permute-done | bytes 8224 | tf_op jit(solution)/shard_map/ppermute | solution.py:450
  16.6 0.0 copy-start.3
  16.6 0.0 copy-done.2
  16.6 0.6 %copy-done.3 = f32[16,128]{1,0:T(8,128)} copy-done((f32[16,128]{1,0:T(8,128)}, f32[16,128]{1,0:T(8,128)S(1)}, u32[]{:S(2)}) %copy-start.3) | copy-done | bytes 8216
  17.2 4.0 %shard_map.108 = (f32[4,512]{1,0:T(4,128)}, f32[16,128]{1,0:T(8,128)}, f32[16,128]{1,0:T(8,128)}, f32[16,128]{1,0:T(8,128)}) custom-call(f32[16,128]{1,0:T(8,128)} %copy-done.2, f32[16,128]{1,0:T(8,128)} %copy-done.3, f32[16,128]{1,0:T(8,128)} %get-tuple-element.29.keep_ref, s32[9,1,128]{2,1,0:T(1,128)} %bitcast.10, f32[9,1,128]{2,1,0:T(1,128)} %bitcast.12, ...), custom_call_target="tpu_custom_call" | custom-call | bytes 65536 | tf_op jit(solution)/shard_map/pallas_call | solution.py:37
  21.1 0.0 collective-permute-start.4
  21.2 0.1 collective-permute-start.5
  21.2 1.3 %collective-permute-done.4.refs_0_ = f32[16,128]{1,0:T(8,128)S(1)} collective-permute-done((f32[16,128]{1,0:T(8,128)}, f32[16,128]{1,0:T(8,128)S(1)}, u32[]{:S(2)}, u32[]{:S(2)}) %collective-permute-start.4) | collective-permute-done | bytes 8224 | tf_op jit(solution)/shard_map/ppermute | solution.py:479
  22.5 0.0 copy-start.6
  22.5 2.6 %collective-permute-done.5.refs_1_ = f32[16,128]{1,0:T(8,128)S(1)} collective-permute-done((f32[16,128]{1,0:T(8,128)}, f32[16,128]{1,0:T(8,128)S(1)}, u32[]{:S(2)}, u32[]{:S(2)}) %collective-permute-start.5) | collective-permute-done | bytes 8224 | tf_op jit(solution)/shard_map/ppermute | solution.py:480
  25.1 0.0 copy-start.7
  25.1 0.0 copy-done.6
  25.1 0.6 %copy-done.7 = f32[16,128]{1,0:T(8,128)} copy-done((f32[16,128]{1,0:T(8,128)}, f32[16,128]{1,0:T(8,128)S(1)}, u32[]{:S(2)}) %copy-start.7) | copy-done | bytes 8216
  25.7 1.4 %shard_map.109 = (f32[16,128]{1,0:T(8,128)}, f32[16,128]{1,0:T(8,128)}, f32[16,128]{1,0:T(8,128)}) custom-call(f32[16,128]{1,0:T(8,128)} %copy-done.6, f32[16,128]{1,0:T(8,128)} %copy-done.7, f32[16,128]{1,0:T(8,128)} %get-tuple-element.39.refs_2_), custom_call_target="tpu_custom_call" | custom-call | bytes 65536 | tf_op jit(solution)/shard_map/pallas_call | solution.py:37
  27.0 0.0 collective-permute-start.6
  27.1 2.7 %collective-permute-start.7 = (f32[16,128]{1,0:T(8,128)}, f32[16,128]{1,0:T(8,128)S(1)}, u32[]{:S(2)}, u32[]{:S(2)}) collective-permute-start(f32[16,128]{1,0:T(8,128)} %get-tuple-element.41), channel_id=1, source_target_pairs={{0,16},{1,2},{2,1},{3,4},{4,3},{5,6},{6,5},{7,8},{8,7},{9,10},{10,... | collective-permute-start | bytes 24584 | tf_op jit(solution)/shard_map/ppermute | solution.py:485
  29.8 2.2 %shard_map.110.ocean_ref = f32[512,128]{1,0:T(8,128)} custom-call(f32[512,128]{1,0:T(8,128)} %bitcast.7, f32[80,128]{1,0:T(8,128)} %copy-done, f32[80,128]{1,0:T(8,128)} %copy-done.1, f32[16,128]{1,0:T(8,128)} %copy-done.2, f32[16,128]{1,0:T(8,128)} %copy-done.3), custom_call_target="tpu_custom_call" | custom-call | tf_op jit(solution)/shard_map/pallas_call | solution.py:486
  31.9 0.0 collective-permute-done.6.got_even_ref
  31.9 0.0 copy-start.4
  31.9 1.1 %collective-permute-done.7.got_odd_ref = f32[16,128]{1,0:T(8,128)S(1)} collective-permute-done((f32[16,128]{1,0:T(8,128)}, f32[16,128]{1,0:T(8,128)S(1)}, u32[]{:S(2)}, u32[]{:S(2)}) %collective-permute-start.7) | collective-permute-done | bytes 8224 | tf_op jit(solution)/shard_map/ppermute | solution.py:485
  33.0 0.0 copy-start.5
  33.0 0.0 copy-done.4
  33.0 0.6 %copy-done.5 = f32[16,128]{1,0:T(8,128)} copy-done((f32[16,128]{1,0:T(8,128)}, f32[16,128]{1,0:T(8,128)S(1)}, u32[]{:S(2)}) %copy-start.5) | copy-done | bytes 8216
  33.6 2.0 %shard_map.111 = f32[512,128]{1,0:T(8,128)} custom-call(f32[16,128]{1,0:T(8,128)} %copy-done.4, f32[16,128]{1,0:T(8,128)} %copy-done.5, f32[16,128]{1,0:T(8,128)} %get-tuple-element.42.keep_ref, s32[9,1,128]{2,1,0:T(1,128)} %bitcast.14, f32[512,128]{1,0:T(8,128)} %shard_map.110.ocean_ref), custom_call_target="tpu_custom_call" | custom-call | bytes 65536 | tf_op jit(solution)/shard_map/pallas_call | solution.py:37
Async XLA Ops:
  2.4 3.8 %collective-permute-start = (f32[80,128]{1,0:T(8,128)}, f32[80,128]{1,0:T(8,128)S(1)}, u32[]{:S(2)}, u32[]{:S(2)}) collective-permute-start(f32[80,128]{1,0:T(8,128)} %get-tuple-element.23), channel_id=1, source_target_pairs={{0,16},{1,17},{2,18},{3,19},{4,20},{5,21},{6,22},{7,23},{8,24},{9,... | collective-permute-start | bytes 122888 | tf_op jit(solution)/shard_map/ppermute | solution.py:436
  2.4 4.2 %collective-permute-start.1 = (f32[80,128]{1,0:T(8,128)}, f32[80,128]{1,0:T(8,128)S(1)}, u32[]{:S(2)}, u32[]{:S(2)}) collective-permute-start(f32[80,128]{1,0:T(8,128)} %get-tuple-element.24), channel_id=1, source_target_pairs={{0,1},{1,0},{2,3},{3,2},{4,5},{5,4},{6,7},{7,6},{8,9},{9,8},{10,11... | collective-permute-start | bytes 122888 | tf_op jit(solution)/shard_map/ppermute | solution.py:437
  6.2 0.6 %copy-start = (f32[80,128]{1,0:T(8,128)}, f32[80,128]{1,0:T(8,128)S(1)}, u32[]{:S(2)}) copy-start(f32[80,128]{1,0:T(8,128)S(1)} %collective-permute-done.refs_0_.x_even_ref) | copy-start | bytes 122884
  6.6 0.6 %copy-start.1 = (f32[80,128]{1,0:T(8,128)}, f32[80,128]{1,0:T(8,128)S(1)}, u32[]{:S(2)}) copy-start(f32[80,128]{1,0:T(8,128)S(1)} %collective-permute-done.1.refs_1_.x_odd_ref) | copy-start | bytes 122884
  8.7 6.9 %collective-permute-start.2 = (f32[16,128]{1,0:T(8,128)}, f32[16,128]{1,0:T(8,128)S(1)}, u32[]{:S(2)}, u32[]{:S(2)}) collective-permute-start(f32[16,128]{1,0:T(8,128)} %get-tuple-element.27), channel_id=1, source_target_pairs={{0,1},{1,0},{2,3},{3,2},{4,5},{5,4},{6,7},{7,6},{8,9},{9,8},{10,11... | collective-permute-start | bytes 24584 | tf_op jit(solution)/shard_map/ppermute | solution.py:449
  10.6 6.0 %collective-permute-start.3 = (f32[16,128]{1,0:T(8,128)}, f32[16,128]{1,0:T(8,128)S(1)}, u32[]{:S(2)}, u32[]{:S(2)}) collective-permute-start(f32[16,128]{1,0:T(8,128)} %get-tuple-element.28), channel_id=1, source_target_pairs={{0,16},{1,2},{2,1},{3,4},{4,3},{5,6},{6,5},{7,8},{8,7},{9,10},{10,... | collective-permute-start | bytes 24584 | tf_op jit(solution)/shard_map/ppermute | solution.py:450
  15.6 1.0 %copy-start.2 = (f32[16,128]{1,0:T(8,128)}, f32[16,128]{1,0:T(8,128)S(1)}, u32[]{:S(2)}) copy-start(f32[16,128]{1,0:T(8,128)S(1)} %collective-permute-done.2.got_even_ref.y_even_ref) | copy-start | bytes 24580
  16.6 0.6 %copy-start.3 = (f32[16,128]{1,0:T(8,128)}, f32[16,128]{1,0:T(8,128)S(1)}, u32[]{:S(2)}) copy-start(f32[16,128]{1,0:T(8,128)S(1)} %collective-permute-done.3.got_odd_ref.y_odd_ref) | copy-start | bytes 24580
  21.1 1.4 %collective-permute-start.4 = (f32[16,128]{1,0:T(8,128)}, f32[16,128]{1,0:T(8,128)S(1)}, u32[]{:S(2)}, u32[]{:S(2)}) collective-permute-start(f32[16,128]{1,0:T(8,128)} %get-tuple-element.37), channel_id=1, source_target_pairs={{0,16},{1,17},{2,18},{3,19},{4,20},{5,21},{6,22},{7,23},{8,24},{9,... | collective-permute-start | bytes 24584 | tf_op jit(solution)/shard_map/ppermute | solution.py:479
  21.2 3.9 %collective-permute-start.5 = (f32[16,128]{1,0:T(8,128)}, f32[16,128]{1,0:T(8,128)S(1)}, u32[]{:S(2)}, u32[]{:S(2)}) collective-permute-start(f32[16,128]{1,0:T(8,128)} %get-tuple-element.38), channel_id=1, source_target_pairs={{0,1},{1,0},{2,3},{3,2},{4,5},{5,4},{6,7},{7,6},{8,9},{9,8},{10,11... | collective-permute-start | bytes 24584 | tf_op jit(solution)/shard_map/ppermute | solution.py:480
  22.5 2.6 %copy-start.6 = (f32[16,128]{1,0:T(8,128)}, f32[16,128]{1,0:T(8,128)S(1)}, u32[]{:S(2)}) copy-start(f32[16,128]{1,0:T(8,128)S(1)} %collective-permute-done.4.refs_0_) | copy-start | bytes 24580
  25.1 0.6 %copy-start.7 = (f32[16,128]{1,0:T(8,128)}, f32[16,128]{1,0:T(8,128)S(1)}, u32[]{:S(2)}) copy-start(f32[16,128]{1,0:T(8,128)S(1)} %collective-permute-done.5.refs_1_) | copy-start | bytes 24580
  27.0 4.9 %collective-permute-start.6 = (f32[16,128]{1,0:T(8,128)}, f32[16,128]{1,0:T(8,128)S(1)}, u32[]{:S(2)}, u32[]{:S(2)}) collective-permute-start(f32[16,128]{1,0:T(8,128)} %get-tuple-element.40), channel_id=1, source_target_pairs={{0,1},{1,0},{2,3},{3,2},{4,5},{5,4},{6,7},{7,6},{8,9},{9,8},{10,11... | collective-permute-start | bytes 24584 | tf_op jit(solution)/shard_map/ppermute | solution.py:484
  27.1 6.0 %collective-permute-start.7 = (f32[16,128]{1,0:T(8,128)}, f32[16,128]{1,0:T(8,128)S(1)}, u32[]{:S(2)}, u32[]{:S(2)}) collective-permute-start(f32[16,128]{1,0:T(8,128)} %get-tuple-element.41), channel_id=1, source_target_pairs={{0,16},{1,2},{2,1},{3,4},{4,3},{5,6},{6,5},{7,8},{8,7},{9,10},{10,... | collective-permute-start | bytes 24584 | tf_op jit(solution)/shard_map/ppermute | solution.py:485
  31.9 1.1 %copy-start.4 = (f32[16,128]{1,0:T(8,128)}, f32[16,128]{1,0:T(8,128)S(1)}, u32[]{:S(2)}) copy-start(f32[16,128]{1,0:T(8,128)S(1)} %collective-permute-done.6.got_even_ref) | copy-start | bytes 24580
  33.0 0.6 %copy-start.5 = (f32[16,128]{1,0:T(8,128)}, f32[16,128]{1,0:T(8,128)S(1)}, u32[]{:S(2)}) copy-start(f32[16,128]{1,0:T(8,128)S(1)} %collective-permute-done.7.got_odd_ref) | copy-start | bytes 24580

commit v2 on v1

--- a/solution.py
+++ b/solution.py
@@ -31,6 +31,7 @@
 HALINE_CONTR = 0.8
 AXES = ("ocx", "ocy")
 VMEM_SPEC = pl.BlockSpec(memory_space=pltpu.VMEM)
+GRANT = pltpu.CompilerParams(vmem_limit_bytes=8 << 20)
 
 
 def call(kernel, outs, *args, cost=0):
@@ -40,6 +41,7 @@
         in_specs=[VMEM_SPEC] * len(args),
         out_specs=jax.tree.map(lambda _: VMEM_SPEC, outs),
         cost_estimate=pl.CostEstimate(flops=cost, bytes_accessed=1 << 16, transcendentals=0),
+        compiler_params=GRANT,
     )(*args)
 
 
@@ -489,6 +491,7 @@
             in_specs=[VMEM_SPEC] * 5,
             out_specs=VMEM_SPEC,
             scratch_shapes=[pltpu.VMEM((64, 128), F32), pltpu.VMEM((64, 128), F32)],
+            compiler_params=GRANT,
         )(ocean, ge_x, go_x, ge_y, go_y)
         ocean_next = call(forcing_kernel, shaped(4 * LEV * 8, 128), he_y, ho_y, keep, cell, moved)
         return (ocean_next.reshape(ocean_state.shape), floe_next)

time: 36 us -> 27.8 us (0.77)
  Pallas kernels: 16.9 us -> 5.32 us
  waiting for transfers between devices: 6.34 us -> 10.2 us
  local copies, waits for them, and re-layouts: 2.39 us -> 1.67 us
    pallas_call x7, Pallas kernels: 14.7 us -> 4.82 us  [call(): pl.pallas_call(kernel, out_shape=outs, in_specs=[VMEM_SPEC] * len(args),...]
    pallas_call x1, Pallas kernels: 2.18 us -> 0.49 us  [body(): pl.pallas_call(ocean_kernel, out_shape=shaped(4 * LEV * 8, 128), in_specs...]
    ppermute x1, waiting for transfers between devices: 0.4 us -> 1.74 us  [body(): go_x = lax.ppermute(send_odd, AXES, x_odd)]
    ppermute x1, waiting for transfers between devices: 1.01 us -> 2.28 us  [body(): go_y = lax.ppermute(send_odd, AXES, y_odd)]
    ppermute x1, waiting for transfers between devices: 1.08 us -> 2.2 us  [body(): ho_y = lax.ppermute(send_odd, AXES, y_odd)]
    unnamed x16 -> x22, local copies, waits for them, and re-layouts: 2.39 us -> 1.67 us
  transfers between devices with their start and end apart: 8 -> 8, of which waited for: 5 -> 6; matrix products, arithmetic and copies ran while one was open for 0% -> 0% of each run, Pallas kernels for 18% -> 6%
where the time goes in v2:
time: 27.8 us; the launch traced here: 27.6 us
  waiting for transfers between devices  10.2 us (37%)
  starting transfers between devices  9.66 us (35%)
  Pallas kernels  5.32 us (19%)
  local copies, waits for them, and re-layouts  1.67 us (6%)
  between operations  0.73 us (3%)
    pallas_call x7, Pallas kernels, call(): pl.pallas_call(kernel, out_shape=outs, in_specs=[VMEM_SPEC] * len(args),...  4.82 us
    ppermute x1, starting transfers between devices, body(): ho_y = lax.ppermute(send_odd, AXES, y_odd)  2.78 us
    ppermute x1, starting transfers between devices, body(): go_y = lax.ppermute(send_odd, AXES, y_odd)  2.7 us
    ppermute x1, waiting for transfers between devices, body(): ho_x = lax.ppermute(send_odd, AXES, x_odd)  2.48 us
    ppermute x1, waiting for transfers between devices, body(): go_y = lax.ppermute(send_odd, AXES, y_odd)  2.28 us
    ppermute x1, waiting for transfers between devices, body(): ho_y = lax.ppermute(send_odd, AXES, y_odd)  2.2 us
    ppermute x1, starting transfers between devices, body(): ge_y = lax.ppermute(send_even, AXES, y_even)  2 us
    ppermute x1, starting transfers between devices, body(): go_x = lax.ppermute(send_odd, AXES, x_odd)  2 us
  transfers between devices with their start and end apart: 8, of which 6 were waited for; matrix products, arithmetic and copies ran while one was open for 0% of the time, Pallas kernels for 6%

profile of v2, /device:TPU:24, one launch (start us, length us, event | category | flops | bytes accessed | tf_op | source)
XLA Modules:
  0.0 27.6 jit_solution(1410882496043433464)
XLA Ops:
  0.6 0.0 copy-start
  0.6 0.9 %copy-done = f32[4,16,8,128]{3,2,1,0:T(8,128)S(1)} copy-done((f32[4,16,8,128]{3,2,1,0:T(8,128)S(1)}, f32[4,16,8,128]{3,2,1,0:T(8,128)}, u32[]{:S(2)}) %copy-start) | copy-done | bytes 262168
  1.6 0.0 copy-start.6
  1.6 0.7 %copy-done.6 = s32[1,9,128]{2,0,1:T(1,128)S(1)} copy-done((s32[1,9,128]{2,0,1:T(1,128)S(1)}, s32[1,9,128]{2,0,1:T(1,128)}, u32[]{:S(2)}) %copy-start.6) | copy-done | bytes 4632
  2.3 0.0 copy-start.4
  2.3 0.0 copy-start.5
  2.3 0.2 shard_map.104
  2.5 0.0 copy-start.2
  2.5 0.1 collective-permute-start
  2.6 2.0 %collective-permute-start.1 = (f32[80,128]{1,0:T(8,128)S(1)}, f32[80,128]{1,0:T(8,128)S(1)}, u32[]{:S(2)}, u32[]{:S(2)}) collective-permute-start(f32[80,128]{1,0:T(8,128)S(1)} %get-tuple-element.24), channel_id=1, source_target_pairs={{0,1},{1,0},{2,3},{3,2},{4,5},{5,4},{6,7},{7,6},{8,9},{9,8},{10,11... | collective-permute-start | bytes 122888 | tf_op jit(solution)/shard_map/ppermute | solution.py:439
  4.6 0.0 copy-done.4
  4.6 0.0 copy-done.5
  4.6 0.0 copy-done.2
  4.6 0.3 %shard_map.105 = (f32[8,128]{1,0:T(8,128)S(1)}, bf16[128,1152]{1,0:T(8,128)(2,1)S(1)}, f32[8,128]{1,0:T(8,128)S(1)}, f32[1,1152]{1,0:T(1,128)S(1)}) custom-call(f32[512,128]{1,0:T(8,128)S(1)} %bitcast.6, s32[9,1,128]{2,1,0:T(1,128)S(1)} %bitcast.8, f32[9,1,128]{2,1,0:T(1,128)S(1)} %bitcast.10, f32[2,512]{1,0:T(2,128)S(1)} %copy-done.2), custom_call_target="tpu_custom_call" | custom-call | bytes 65536 | tf_op jit(solution)/shard_map/pallas_call | solution.py:38
  4.9 0.0 collective-permute-done.refs_0_.x_even_ref
  4.9 1.7 %collective-permute-done.1.refs_1_.x_odd_ref = f32[80,128]{1,0:T(8,128)S(1)} collective-permute-done((f32[80,128]{1,0:T(8,128)S(1)}, f32[80,128]{1,0:T(8,128)S(1)}, u32[]{:S(2)}, u32[]{:S(2)}) %collective-permute-start.1) | collective-permute-done | bytes 40992 | tf_op jit(solution)/shard_map/ppermute | solution.py:439
  6.7 0.0 copy-start.3
  6.7 0.0 copy-start.8
  6.7 0.0 copy-start.9
  6.7 0.0 copy-start.10
  6.7 2.0 %collective-permute-start.2 = (f32[16,128]{1,0:T(8,128)S(1)}, f32[16,128]{1,0:T(8,128)S(1)}, u32[]{:S(2)}, u32[]{:S(2)}) collective-permute-start(f32[16,128]{1,0:T(8,128)S(1)} %get-tuple-element.27), channel_id=1, source_target_pairs={{0,1},{1,0},{2,3},{3,2},{4,5},{5,4},{6,7},{7,6},{8,9},{9,8},{10,11... | collective-permute-start | bytes 24584 | tf_op jit(solution)/shard_map/ppermute | solution.py:451
  8.7 2.7 %collective-permute-start.3 = (f32[16,128]{1,0:T(8,128)S(1)}, f32[16,128]{1,0:T(8,128)S(1)}, u32[]{:S(2)}, u32[]{:S(2)}) collective-permute-start(f32[16,128]{1,0:T(8,128)S(1)} %get-tuple-element.28), channel_id=1, source_target_pairs={{0,16},{1,2},{2,1},{3,4},{4,3},{5,6},{6,5},{7,8},{8,7},{9,10},{10,... | collective-permute-start | bytes 24584 | tf_op jit(solution)/shard_map/ppermute | solution.py:452
  11.4 0.0 copy-done.3
  11.4 0.0 copy-done.8
  11.4 0.0 copy-done.9
  11.4 0.0 copy-done.10
  11.4 0.7 %shard_map.107 = (f32[4,128,128]{2,1,0:T(8,128)S(1)}, f32[4,128,128]{2,1,0:T(8,128)S(1)}, f32[4,128,128]{2,1,0:T(8,128)S(1)}, f32[8,128]{1,0:T(8,128)S(1)}) custom-call(s32[2,4,512]{2,1,0:T(4,128)S(1)} %copy-done.8, s32[2,4,256]{2,1,0:T(4,128)S(1)} %copy-done.9, s32[4,256]{1,0:T(4,128)S(1)} %copy-done.10, f32[2,512]{1,0:T(2,128)S(1)} %copy-done.2, ...), custom_call_target="tpu_custom_call" | custom-call | bytes 65536 | tf_op jit(solution)/shard_map/pallas_call | solution.py:38
  12.2 0.0 collective-permute-done.2.got_even_ref.y_even_ref
  12.2 2.3 %collective-permute-done.3.got_odd_ref.y_odd_ref = f32[16,128]{1,0:T(8,128)S(1)} collective-permute-done((f32[16,128]{1,0:T(8,128)S(1)}, f32[16,128]{1,0:T(8,128)S(1)}, u32[]{:S(2)}, u32[]{:S(2)}) %collective-permute-start.3) | collective-permute-done | bytes 8224 | tf_op jit(solution)/shard_map/ppermute | solution.py:452
  14.5 0.0 copy-start.1
  14.5 2.5 %shard_map.108 = (f32[4,512]{1,0:T(4,128)}, f32[16,128]{1,0:T(8,128)S(1)}, f32[16,128]{1,0:T(8,128)S(1)}, f32[16,128]{1,0:T(8,128)S(1)}) custom-call(f32[16,128]{1,0:T(8,128)S(1)} %collective-permute-done.2.got_even_ref.y_even_ref, f32[16,128]{1,0:T(8,128)S(1)} %collective-permute-done.3.got_odd_ref.y_odd_ref, f32[16,128]{1,0:T(8,128)S(1)} %get-tuple-element.29.keep_ref, ...), custom_call_target="tpu_custom_call" | custom-call | bytes 65536 | tf_op jit(solution)/shard_map/pallas_call | solution.py:38
  17.0 0.0 collective-permute-start.4
  17.0 0.0 collective-permute-start.5
  17.0 1.2 %collective-permute-done.4.refs_0_ = f32[16,128]{1,0:T(8,128)S(1)} collective-permute-done((f32[16,128]{1,0:T(8,128)S(1)}, f32[16,128]{1,0:T(8,128)S(1)}, u32[]{:S(2)}, u32[]{:S(2)}) %collective-permute-start.4) | collective-permute-done | bytes 8224 | tf_op jit(solution)/shard_map/ppermute | solution.py:481
  18.2 2.5 %collective-permute-done.5.refs_1_ = f32[16,128]{1,0:T(8,128)S(1)} collective-permute-done((f32[16,128]{1,0:T(8,128)S(1)}, f32[16,128]{1,0:T(8,128)S(1)}, u32[]{:S(2)}, u32[]{:S(2)}) %collective-permute-start.5) | collective-permute-done | bytes 8224 | tf_op jit(solution)/shard_map/ppermute | solution.py:482
  20.7 0.1 collective-permute-start.6
  20.8 2.8 %collective-permute-start.7 = (f32[16,128]{1,0:T(8,128)S(1)}, f32[16,128]{1,0:T(8,128)S(1)}, u32[]{:S(2)}, u32[]{:S(2)}) collective-permute-start(f32[16,128]{1,0:T(8,128)S(1)} %get-tuple-element.41), channel_id=1, source_target_pairs={{0,16},{1,2},{2,1},{3,4},{4,3},{5,6},{6,5},{7,8},{8,7},{9,10},{10,... | collective-permute-start | bytes 24584 | tf_op jit(solution)/shard_map/ppermute | solution.py:487
  23.6 0.0 copy-done.1
  23.6 0.0 copy-start.7
  23.6 0.5 %shard_map.110.ocean_ref = f32[512,128]{1,0:T(8,128)S(1)} custom-call(f32[512,128]{1,0:T(8,128)S(1)} %bitcast.7, f32[80,128]{1,0:T(8,128)S(1)} %collective-permute-done.refs_0_.x_even_ref, f32[80,128]{1,0:T(8,128)S(1)} %collective-permute-done.1.refs_1_.x_odd_ref, f32[16,128]{1,0:T(8,128)S(1)} %collective-permute-done.2.got_even_ref.y_even_ref, ...), custom_call_target="tpu_custom_call" | custom-call | tf_op jit(solution)/shard_map/pallas_call | solution.py:488
  24.1 0.4 %collective-permute-done.6.got_even_ref = f32[16,128]{1,0:T(8,128)S(1)} collective-permute-done((f32[16,128]{1,0:T(8,128)S(1)}, f32[16,128]{1,0:T(8,128)S(1)}, u32[]{:S(2)}, u32[]{:S(2)}) %collective-permute-start.6) | collective-permute-done | bytes 8224 | tf_op jit(solution)/shard_map/ppermute | solution.py:486
  24.4 2.2 %collective-permute-done.7.got_odd_ref = f32[16,128]{1,0:T(8,128)S(1)} collective-permute-done((f32[16,128]{1,0:T(8,128)S(1)}, f32[16,128]{1,0:T(8,128)S(1)}, u32[]{:S(2)}, u32[]{:S(2)}) %collective-permute-start.7) | collective-permute-done | bytes 8224 | tf_op jit(solution)/shard_map/ppermute | solution.py:487
  26.6 0.0 copy-done.7
  26.6 1.0 %shard_map.111 = f32[512,128]{1,0:T(8,128)} custom-call(f32[16,128]{1,0:T(8,128)S(1)} %collective-permute-done.6.got_even_ref, f32[16,128]{1,0:T(8,128)S(1)} %collective-permute-done.7.got_odd_ref, f32[16,128]{1,0:T(8,128)S(1)} %get-tuple-element.42.keep_ref, s32[9,1,128]{2,1,0:T(1,128)S(1)} %bitcast.13, f32[512,128]{1,0:T(8,128)S(1)} %shard_map.110.ocean_ref), custom_call_target="tpu_custom_call" | custom-call | bytes 65536 | tf_op jit(solution)/shard_map/pallas_call | solution.py:38
  (2 shorter events, 0.0 us)
Async XLA Ops:
  0.6 1.0 %copy-start = (f32[4,16,8,128]{3,2,1,0:T(8,128)S(1)}, f32[4,16,8,128]{3,2,1,0:T(8,128)}, u32[]{:S(2)}) copy-start(f32[4,16,8,128]{3,2,1,0:T(8,128)} %param.9) | copy-start | bytes 786436
  1.6 0.7 %copy-start.6 = (s32[1,9,128]{2,0,1:T(1,128)S(1)}, s32[1,9,128]{2,0,1:T(1,128)}, u32[]{:S(2)}) copy-start(s32[1,9,128]{2,0,1:T(1,128)} %param.17) | copy-start | bytes 13828
  2.3 2.3 %copy-start.4 = (s32[1,9,128]{2,0,1:T(1,128)S(1)}, s32[1,9,128]{2,0,1:T(1,128)}, u32[]{:S(2)}) copy-start(s32[1,9,128]{2,0,1:T(1,128)} %param.15) | copy-start | bytes 13828
  2.3 2.3 %copy-start.5 = (f32[1,9,128]{2,0,1:T(1,128)S(1)}, f32[1,9,128]{2,0,1:T(1,128)}, u32[]{:S(2)}) copy-start(f32[1,9,128]{2,0,1:T(1,128)} %param.16) | copy-start | bytes 13828
  2.5 2.1 %copy-start.2 = (f32[2,512]{1,0:T(2,128)S(1)}, f32[2,512]{1,0:T(2,128)}, u32[]{:S(2)}) copy-start(f32[2,512]{1,0:T(2,128)} %props_ref.5) | copy-start | bytes 12292
  2.5 2.4 %collective-permute-start = (f32[80,128]{1,0:T(8,128)S(1)}, f32[80,128]{1,0:T(8,128)S(1)}, u32[]{:S(2)}, u32[]{:S(2)}) collective-permute-start(f32[80,128]{1,0:T(8,128)S(1)} %get-tuple-element.23), channel_id=1, source_target_pairs={{0,16},{1,17},{2,18},{3,19},{4,20},{5,21},{6,22},{7,23},{8,24},{9,... | collective-permute-start | bytes 122888 | tf_op jit(solution)/shard_map/ppermute | solution.py:438
  2.6 4.1 %collective-permute-start.1 = (f32[80,128]{1,0:T(8,128)S(1)}, f32[80,128]{1,0:T(8,128)S(1)}, u32[]{:S(2)}, u32[]{:S(2)}) collective-permute-start(f32[80,128]{1,0:T(8,128)S(1)} %get-tuple-element.24), channel_id=1, source_target_pairs={{0,1},{1,0},{2,3},{3,2},{4,5},{5,4},{6,7},{7,6},{8,9},{9,8},{10,11... | collective-permute-start | bytes 122888 | tf_op jit(solution)/shard_map/ppermute | solution.py:439
  6.7 4.7 %copy-start.3 = (f32[4,512]{1,0:T(4,128)S(1)}, f32[4,512]{1,0:T(4,128)}, u32[]{:S(2)}) copy-start(f32[4,512]{1,0:T(4,128)} %state_ref.3) | copy-start | bytes 24580
  6.7 4.7 %copy-start.8 = (s32[2,4,512]{2,1,0:T(4,128)S(1)}, s32[2,4,512]{2,1,0:T(4,128)}, u32[]{:S(2)}) copy-start(s32[2,4,512]{2,1,0:T(4,128)} %pairs_ref.1) | copy-start | bytes 49156
  6.7 4.7 %copy-start.9 = (s32[2,4,256]{2,1,0:T(4,128)S(1)}, s32[2,4,256]{2,1,0:T(4,128)}, u32[]{:S(2)}) copy-start(s32[2,4,256]{2,1,0:T(4,128)} %bonds_ref.1) | copy-start | bytes 24580
  6.7 4.7 %copy-start.10 = (s32[4,256]{1,0:T(4,128)S(1)}, s32[4,256]{1,0:T(4,128)}, u32[]{:S(2)}) copy-start(s32[4,256]{1,0:T(4,128)} %broken_ref.1) | copy-start | bytes 12292
  6.7 5.5 %collective-permute-start.2 = (f32[16,128]{1,0:T(8,128)S(1)}, f32[16,128]{1,0:T(8,128)S(1)}, u32[]{:S(2)}, u32[]{:S(2)}) collective-permute-start(f32[16,128]{1,0:T(8,128)S(1)} %get-tuple-element.27), channel_id=1, source_target_pairs={{0,1},{1,0},{2,3},{3,2},{4,5},{5,4},{6,7},{7,6},{8,9},{9,8},{10,11... | collective-permute-start | bytes 24584 | tf_op jit(solution)/shard_map/ppermute | solution.py:451
  8.7 5.8 %collective-permute-start.3 = (f32[16,128]{1,0:T(8,128)S(1)}, f32[16,128]{1,0:T(8,128)S(1)}, u32[]{:S(2)}, u32[]{:S(2)}) collective-permute-start(f32[16,128]{1,0:T(8,128)S(1)} %get-tuple-element.28), channel_id=1, source_target_pairs={{0,16},{1,2},{2,1},{3,4},{4,3},{5,6},{6,5},{7,8},{8,7},{9,10},{10,... | collective-permute-start | bytes 24584 | tf_op jit(solution)/shard_map/ppermute | solution.py:452
  14.5 9.1 %copy-start.1 = (f32[4,16,8,128]{3,2,1,0:T(8,128)S(1)}, f32[4,16,8,128]{3,2,1,0:T(8,128)}, u32[]{:S(2)}) copy-start(f32[4,16,8,128]{3,2,1,0:T(8,128)} %param.9) | copy-start | bytes 786436
  17.0 1.2 %collective-permute-start.4 = (f32[16,128]{1,0:T(8,128)S(1)}, f32[16,128]{1,0:T(8,128)S(1)}, u32[]{:S(2)}, u32[]{:S(2)}) collective-permute-start(f32[16,128]{1,0:T(8,128)S(1)} %get-tuple-element.37), channel_id=1, source_target_pairs={{0,16},{1,17},{2,18},{3,19},{4,20},{5,21},{6,22},{7,23},{8,24},{9,... | collective-permute-start | bytes 24584 | tf_op jit(solution)/shard_map/ppermute | solution.py:481
  17.0 3.7 %collective-permute-start.5 = (f32[16,128]{1,0:T(8,128)S(1)}, f32[16,128]{1,0:T(8,128)S(1)}, u32[]{:S(2)}, u32[]{:S(2)}) collective-permute-start(f32[16,128]{1,0:T(8,128)S(1)} %get-tuple-element.38), channel_id=1, source_target_pairs={{0,1},{1,0},{2,3},{3,2},{4,5},{5,4},{6,7},{7,6},{8,9},{9,8},{10,11... | collective-permute-start | bytes 24584 | tf_op jit(solution)/shard_map/ppermute | solution.py:482
  20.7 3.7 %collective-permute-start.6 = (f32[16,128]{1,0:T(8,128)S(1)}, f32[16,128]{1,0:T(8,128)S(1)}, u32[]{:S(2)}, u32[]{:S(2)}) collective-permute-start(f32[16,128]{1,0:T(8,128)S(1)} %get-tuple-element.40), channel_id=1, source_target_pairs={{0,1},{1,0},{2,3},{3,2},{4,5},{5,4},{6,7},{7,6},{8,9},{9,8},{10,11... | collective-permute-start | bytes 24584 | tf_op jit(solution)/shard_map/ppermute | solution.py:486
  20.8 5.8 %collective-permute-start.7 = (f32[16,128]{1,0:T(8,128)S(1)}, f32[16,128]{1,0:T(8,128)S(1)}, u32[]{:S(2)}, u32[]{:S(2)}) collective-permute-start(f32[16,128]{1,0:T(8,128)S(1)} %get-tuple-element.41), channel_id=1, source_target_pairs={{0,16},{1,2},{2,1},{3,4},{4,3},{5,6},{6,5},{7,8},{8,7},{9,10},{10,... | collective-permute-start | bytes 24584 | tf_op jit(solution)/shard_map/ppermute | solution.py:487
  23.6 3.1 %copy-start.7 = (s32[1,9,128]{2,0,1:T(1,128)S(1)}, s32[1,9,128]{2,0,1:T(1,128)}, u32[]{:S(2)}) copy-start(s32[1,9,128]{2,0,1:T(1,128)} %param.17) | copy-start | bytes 13828

commit v3 on v2

--- a/solution.py
+++ b/solution.py
@@ -9,7 +9,6 @@
 BF16 = jnp.bfloat16
 I32 = jnp.int32
 
-TILE = 128
 TILES = 4
 SUBSTEPS = 4
 LEV = 16
@@ -435,8 +434,8 @@
         send_even, send_odd, own = call(
             sample_kernel, (shaped(80, 128), shaped(80, 128), small), ocean, cell
         )
-        ge_x = lax.ppermute(send_even, AXES, x_even)
-        go_x = lax.ppermute(send_odd, AXES, x_odd)
+        ge_x = exchange(send_even, x_even)
+        go_x = exchange(send_odd, x_odd)
         cols, table, area, salt = call(
             column_kernel,
             (shaped(8, 128), shaped(128, ENTRIES, dtype=BF16), shaped(8, 128), shaped(1, ENTRIES)),
@@ -448,8 +447,8 @@
         send_even, send_odd, keep = call(
             turn_kernel(3, True), (small, small, small), ge_x, go_x, own, cols
         )
-        ge_y = lax.ppermute(send_even, AXES, y_even)
-        go_y = lax.ppermute(send_odd, AXES, y_odd)
+        ge_y = exchange(send_even, y_even)
+        go_y = exchange(send_odd, y_odd)
         square = shaped(TILES, 128, 128)
         reach, contact, bond, force = call(
             pair_kernel,
@@ -478,13 +477,13 @@
             floe_state,
             floe_props,
         )
-        he_x = lax.ppermute(send_even, AXES, x_even)
-        ho_x = lax.ppermute(send_odd, AXES, x_odd)
+        he_x = exchange(send_even, x_even)
+        ho_x = exchange(send_odd, x_odd)
         send_even, send_odd, keep = call(
             turn_kernel(4, False), (small, small, small), he_x, ho_x, own
         )
-        he_y = lax.ppermute(send_even, AXES, y_even)
-        ho_y = lax.ppermute(send_odd, AXES, y_odd)
+        he_y = exchange(send_even, y_even)
+        ho_y = exchange(send_odd, y_odd)
         moved = pl.pallas_call(
             ocean_kernel,
             out_shape=shaped(4 * LEV * 8, 128),
@@ -497,6 +496,10 @@
         return (ocean_next.reshape(ocean_state.shape), floe_next)
 
     return body
+
+
+def exchange(data, pairs):
+    return lax.ppermute(data, AXES, pairs)
 
 
 def solution(mesh):

time: 27.8 us -> 27.8 us (level)
  no operation moved by 1% of the time
where the time goes in v3:
time: 27.8 us; the launch traced here: 27.6 us
  waiting for transfers between devices  10.2 us (37%)
  starting transfers between devices  9.66 us (35%)
  Pallas kernels  5.32 us (19%)
  local copies, waits for them, and re-layouts  1.67 us (6%)
  between operations  0.73 us (3%)
    ppermute x8, waiting for transfers between devices, exchange(): return lax.ppermute(data, AXES, pairs)  10.2 us
    ppermute x8, starting transfers between devices, exchange(): return lax.ppermute(data, AXES, pairs)  9.66 us
    pallas_call x7, Pallas kernels, call(): pl.pallas_call(kernel, out_shape=outs, in_specs=[VMEM_SPEC] * len(args),...  4.82 us
    unnamed x22, local copies, waits for them, and re-layouts  1.67 us
  transfers between devices with their start and end apart: 8, of which 6 were waited for; matrix products, arithmetic and copies ran while one was open for 0% of the time, Pallas kernels for 6%

profile of v3, /device:TPU:24, one launch (start us, length us, event | category | flops | bytes accessed | tf_op | source)
XLA Modules:
  0.0 27.6 jit_solution(1410882496043433464)
XLA Ops:
  0.6 0.0 copy-start
  0.6 0.9 %copy-done = f32[4,16,8,128]{3,2,1,0:T(8,128)S(1)} copy-done((f32[4,16,8,128]{3,2,1,0:T(8,128)S(1)}, f32[4,16,8,128]{3,2,1,0:T(8,128)}, u32[]{:S(2)}) %copy-start) | copy-done | bytes 262168
  1.6 0.0 copy-start.6
  1.6 0.7 %copy-done.6 = s32[1,9,128]{2,0,1:T(1,128)S(1)} copy-done((s32[1,9,128]{2,0,1:T(1,128)S(1)}, s32[1,9,128]{2,0,1:T(1,128)}, u32[]{:S(2)}) %copy-start.6) | copy-done | bytes 4632
  2.3 0.0 copy-start.4
  2.3 0.0 copy-start.5
  2.3 0.2 shard_map.104
  2.5 0.0 copy-start.2
  2.5 0.1 collective-permute-start
  2.6 2.0 %collective-permute-start.1 = (f32[80,128]{1,0:T(8,128)S(1)}, f32[80,128]{1,0:T(8,128)S(1)}, u32[]{:S(2)}, u32[]{:S(2)}) collective-permute-start(f32[80,128]{1,0:T(8,128)S(1)} %get-tuple-element.24), channel_id=1, source_target_pairs={{0,1},{1,0},{2,3},{3,2},{4,5},{5,4},{6,7},{7,6},{8,9},{9,8},{10,11... | collective-permute-start | bytes 122888 | tf_op jit(solution)/shard_map/ppermute | solution.py:502
  4.6 0.0 copy-done.4
  4.6 0.0 copy-done.5
  4.6 0.0 copy-done.2
  4.6 0.3 %shard_map.105 = (f32[8,128]{1,0:T(8,128)S(1)}, bf16[128,1152]{1,0:T(8,128)(2,1)S(1)}, f32[8,128]{1,0:T(8,128)S(1)}, f32[1,1152]{1,0:T(1,128)S(1)}) custom-call(f32[512,128]{1,0:T(8,128)S(1)} %bitcast.6, s32[9,1,128]{2,1,0:T(1,128)S(1)} %bitcast.8, f32[9,1,128]{2,1,0:T(1,128)S(1)} %bitcast.10, f32[2,512]{1,0:T(2,128)S(1)} %copy-done.2), custom_call_target="tpu_custom_call" | custom-call | bytes 65536 | tf_op jit(solution)/shard_map/pallas_call | solution.py:37
  4.9 0.0 collective-permute-done.refs_0_.x_even_ref
  4.9 1.7 %collective-permute-done.1.refs_1_.x_odd_ref = f32[80,128]{1,0:T(8,128)S(1)} collective-permute-done((f32[80,128]{1,0:T(8,128)S(1)}, f32[80,128]{1,0:T(8,128)S(1)}, u32[]{:S(2)}, u32[]{:S(2)}) %collective-permute-start.1) | collective-permute-done | bytes 40992 | tf_op jit(solution)/shard_map/ppermute | solution.py:502
  6.7 0.0 copy-start.3
  6.7 0.0 copy-start.8
  6.7 0.0 copy-start.9
  6.7 0.0 copy-start.10
  6.7 2.0 %collective-permute-start.2 = (f32[16,128]{1,0:T(8,128)S(1)}, f32[16,128]{1,0:T(8,128)S(1)}, u32[]{:S(2)}, u32[]{:S(2)}) collective-permute-start(f32[16,128]{1,0:T(8,128)S(1)} %get-tuple-element.27), channel_id=1, source_target_pairs={{0,1},{1,0},{2,3},{3,2},{4,5},{5,4},{6,7},{7,6},{8,9},{9,8},{10,11... | collective-permute-start | bytes 24584 | tf_op jit(solution)/shard_map/ppermute | solution.py:502
  8.7 2.7 %collective-permute-start.3 = (f32[16,128]{1,0:T(8,128)S(1)}, f32[16,128]{1,0:T(8,128)S(1)}, u32[]{:S(2)}, u32[]{:S(2)}) collective-permute-start(f32[16,128]{1,0:T(8,128)S(1)} %get-tuple-element.28), channel_id=1, source_target_pairs={{0,16},{1,2},{2,1},{3,4},{4,3},{5,6},{6,5},{7,8},{8,7},{9,10},{10,... | collective-permute-start | bytes 24584 | tf_op jit(solution)/shard_map/ppermute | solution.py:502
  11.4 0.0 copy-done.3
  11.4 0.0 copy-done.8
  11.4 0.0 copy-done.9
  11.4 0.0 copy-done.10
  11.4 0.7 %shard_map.107 = (f32[4,128,128]{2,1,0:T(8,128)S(1)}, f32[4,128,128]{2,1,0:T(8,128)S(1)}, f32[4,128,128]{2,1,0:T(8,128)S(1)}, f32[8,128]{1,0:T(8,128)S(1)}) custom-call(s32[2,4,512]{2,1,0:T(4,128)S(1)} %copy-done.8, s32[2,4,256]{2,1,0:T(4,128)S(1)} %copy-done.9, s32[4,256]{1,0:T(4,128)S(1)} %copy-done.10, f32[2,512]{1,0:T(2,128)S(1)} %copy-done.2, ...), custom_call_target="tpu_custom_call" | custom-call | bytes 65536 | tf_op jit(solution)/shard_map/pallas_call | solution.py:37
  12.2 0.0 collective-permute-done.2.got_even_ref.y_even_ref
  12.2 2.3 %collective-permute-done.3.got_odd_ref.y_odd_ref = f32[16,128]{1,0:T(8,128)S(1)} collective-permute-done((f32[16,128]{1,0:T(8,128)S(1)}, f32[16,128]{1,0:T(8,128)S(1)}, u32[]{:S(2)}, u32[]{:S(2)}) %collective-permute-start.3) | collective-permute-done | bytes 8224 | tf_op jit(solution)/shard_map/ppermute | solution.py:502
  14.5 0.0 copy-start.1
  14.5 2.5 %shard_map.108 = (f32[4,512]{1,0:T(4,128)}, f32[16,128]{1,0:T(8,128)S(1)}, f32[16,128]{1,0:T(8,128)S(1)}, f32[16,128]{1,0:T(8,128)S(1)}) custom-call(f32[16,128]{1,0:T(8,128)S(1)} %collective-permute-done.2.got_even_ref.y_even_ref, f32[16,128]{1,0:T(8,128)S(1)} %collective-permute-done.3.got_odd_ref.y_odd_ref, f32[16,128]{1,0:T(8,128)S(1)} %get-tuple-element.29.keep_ref, ...), custom_call_target="tpu_custom_call" | custom-call | bytes 65536 | tf_op jit(solution)/shard_map/pallas_call | solution.py:37
  17.0 0.0 collective-permute-start.4
  17.0 0.0 collective-permute-start.5
  17.0 1.2 %collective-permute-done.4.refs_0_ = f32[16,128]{1,0:T(8,128)S(1)} collective-permute-done((f32[16,128]{1,0:T(8,128)S(1)}, f32[16,128]{1,0:T(8,128)S(1)}, u32[]{:S(2)}, u32[]{:S(2)}) %collective-permute-start.4) | collective-permute-done | bytes 8224 | tf_op jit(solution)/shard_map/ppermute | solution.py:502
  18.2 2.5 %collective-permute-done.5.refs_1_ = f32[16,128]{1,0:T(8,128)S(1)} collective-permute-done((f32[16,128]{1,0:T(8,128)S(1)}, f32[16,128]{1,0:T(8,128)S(1)}, u32[]{:S(2)}, u32[]{:S(2)}) %collective-permute-start.5) | collective-permute-done | bytes 8224 | tf_op jit(solution)/shard_map/ppermute | solution.py:502
  20.7 0.1 collective-permute-start.6
  20.8 2.8 %collective-permute-start.7 = (f32[16,128]{1,0:T(8,128)S(1)}, f32[16,128]{1,0:T(8,128)S(1)}, u32[]{:S(2)}, u32[]{:S(2)}) collective-permute-start(f32[16,128]{1,0:T(8,128)S(1)} %get-tuple-element.41), channel_id=1, source_target_pairs={{0,16},{1,2},{2,1},{3,4},{4,3},{5,6},{6,5},{7,8},{8,7},{9,10},{10,... | collective-permute-start | bytes 24584 | tf_op jit(solution)/shard_map/ppermute | solution.py:502
  23.6 0.0 copy-done.1
  23.6 0.0 copy-start.7
  23.6 0.5 %shard_map.110.ocean_ref = f32[512,128]{1,0:T(8,128)S(1)} custom-call(f32[512,128]{1,0:T(8,128)S(1)} %bitcast.7, f32[80,128]{1,0:T(8,128)S(1)} %collective-permute-done.refs_0_.x_even_ref, f32[80,128]{1,0:T(8,128)S(1)} %collective-permute-done.1.refs_1_.x_odd_ref, f32[16,128]{1,0:T(8,128)S(1)} %collective-permute-done.2.got_even_ref.y_even_ref, ...), custom_call_target="tpu_custom_call" | custom-call | tf_op jit(solution)/shard_map/pallas_call | solution.py:487
  24.1 0.4 %collective-permute-done.6.got_even_ref = f32[16,128]{1,0:T(8,128)S(1)} collective-permute-done((f32[16,128]{1,0:T(8,128)S(1)}, f32[16,128]{1,0:T(8,128)S(1)}, u32[]{:S(2)}, u32[]{:S(2)}) %collective-permute-start.6) | collective-permute-done | bytes 8224 | tf_op jit(solution)/shard_map/ppermute | solution.py:502
  24.4 2.2 %collective-permute-done.7.got_odd_ref = f32[16,128]{1,0:T(8,128)S(1)} collective-permute-done((f32[16,128]{1,0:T(8,128)S(1)}, f32[16,128]{1,0:T(8,128)S(1)}, u32[]{:S(2)}, u32[]{:S(2)}) %collective-permute-start.7) | collective-permute-done | bytes 8224 | tf_op jit(solution)/shard_map/ppermute | solution.py:502
  26.6 0.0 copy-done.7
  26.6 1.0 %shard_map.111 = f32[512,128]{1,0:T(8,128)} custom-call(f32[16,128]{1,0:T(8,128)S(1)} %collective-permute-done.6.got_even_ref, f32[16,128]{1,0:T(8,128)S(1)} %collective-permute-done.7.got_odd_ref, f32[16,128]{1,0:T(8,128)S(1)} %get-tuple-element.42.keep_ref, s32[9,1,128]{2,1,0:T(1,128)S(1)} %bitcast.13, f32[512,128]{1,0:T(8,128)S(1)} %shard_map.110.ocean_ref), custom_call_target="tpu_custom_call" | custom-call | bytes 65536 | tf_op jit(solution)/shard_map/pallas_call | solution.py:37
  (2 shorter events, 0.0 us)
Async XLA Ops:
  0.6 1.0 %copy-start = (f32[4,16,8,128]{3,2,1,0:T(8,128)S(1)}, f32[4,16,8,128]{3,2,1,0:T(8,128)}, u32[]{:S(2)}) copy-start(f32[4,16,8,128]{3,2,1,0:T(8,128)} %param.9) | copy-start | bytes 786436
  1.6 0.7 %copy-start.6 = (s32[1,9,128]{2,0,1:T(1,128)S(1)}, s32[1,9,128]{2,0,1:T(1,128)}, u32[]{:S(2)}) copy-start(s32[1,9,128]{2,0,1:T(1,128)} %param.17) | copy-start | bytes 13828
  2.3 2.3 %copy-start.4 = (s32[1,9,128]{2,0,1:T(1,128)S(1)}, s32[1,9,128]{2,0,1:T(1,128)}, u32[]{:S(2)}) copy-start(s32[1,9,128]{2,0,1:T(1,128)} %param.15) | copy-start | bytes 13828
  2.3 2.3 %copy-start.5 = (f32[1,9,128]{2,0,1:T(1,128)S(1)}, f32[1,9,128]{2,0,1:T(1,128)}, u32[]{:S(2)}) copy-start(f32[1,9,128]{2,0,1:T(1,128)} %param.16) | copy-start | bytes 13828
  2.5 2.1 %copy-start.2 = (f32[2,512]{1,0:T(2,128)S(1)}, f32[2,512]{1,0:T(2,128)}, u32[]{:S(2)}) copy-start(f32[2,512]{1,0:T(2,128)} %props_ref.5) | copy-start | bytes 12292
  2.5 2.4 %collective-permute-start = (f32[80,128]{1,0:T(8,128)S(1)}, f32[80,128]{1,0:T(8,128)S(1)}, u32[]{:S(2)}, u32[]{:S(2)}) collective-permute-start(f32[80,128]{1,0:T(8,128)S(1)} %get-tuple-element.23), channel_id=1, source_target_pairs={{0,16},{1,17},{2,18},{3,19},{4,20},{5,21},{6,22},{7,23},{8,24},{9,... | collective-permute-start | bytes 122888 | tf_op jit(solution)/shard_map/ppermute | solution.py:502
  2.6 4.1 %collective-permute-start.1 = (f32[80,128]{1,0:T(8,128)S(1)}, f32[80,128]{1,0:T(8,128)S(1)}, u32[]{:S(2)}, u32[]{:S(2)}) collective-permute-start(f32[80,128]{1,0:T(8,128)S(1)} %get-tuple-element.24), channel_id=1, source_target_pairs={{0,1},{1,0},{2,3},{3,2},{4,5},{5,4},{6,7},{7,6},{8,9},{9,8},{10,11... | collective-permute-start | bytes 122888 | tf_op jit(solution)/shard_map/ppermute | solution.py:502
  6.7 4.7 %copy-start.3 = (f32[4,512]{1,0:T(4,128)S(1)}, f32[4,512]{1,0:T(4,128)}, u32[]{:S(2)}) copy-start(f32[4,512]{1,0:T(4,128)} %state_ref.3) | copy-start | bytes 24580
  6.7 4.7 %copy-start.8 = (s32[2,4,512]{2,1,0:T(4,128)S(1)}, s32[2,4,512]{2,1,0:T(4,128)}, u32[]{:S(2)}) copy-start(s32[2,4,512]{2,1,0:T(4,128)} %pairs_ref.1) | copy-start | bytes 49156
  6.7 4.7 %copy-start.9 = (s32[2,4,256]{2,1,0:T(4,128)S(1)}, s32[2,4,256]{2,1,0:T(4,128)}, u32[]{:S(2)}) copy-start(s32[2,4,256]{2,1,0:T(4,128)} %bonds_ref.1) | copy-start | bytes 24580
  6.7 4.7 %copy-start.10 = (s32[4,256]{1,0:T(4,128)S(1)}, s32[4,256]{1,0:T(4,128)}, u32[]{:S(2)}) copy-start(s32[4,256]{1,0:T(4,128)} %broken_ref.1) | copy-start | bytes 12292
  6.7 5.5 %collective-permute-start.2 = (f32[16,128]{1,0:T(8,128)S(1)}, f32[16,128]{1,0:T(8,128)S(1)}, u32[]{:S(2)}, u32[]{:S(2)}) collective-permute-start(f32[16,128]{1,0:T(8,128)S(1)} %get-tuple-element.27), channel_id=1, source_target_pairs={{0,1},{1,0},{2,3},{3,2},{4,5},{5,4},{6,7},{7,6},{8,9},{9,8},{10,11... | collective-permute-start | bytes 24584 | tf_op jit(solution)/shard_map/ppermute | solution.py:502
  8.7 5.8 %collective-permute-start.3 = (f32[16,128]{1,0:T(8,128)S(1)}, f32[16,128]{1,0:T(8,128)S(1)}, u32[]{:S(2)}, u32[]{:S(2)}) collective-permute-start(f32[16,128]{1,0:T(8,128)S(1)} %get-tuple-element.28), channel_id=1, source_target_pairs={{0,16},{1,2},{2,1},{3,4},{4,3},{5,6},{6,5},{7,8},{8,7},{9,10},{10,... | collective-permute-start | bytes 24584 | tf_op jit(solution)/shard_map/ppermute | solution.py:502
  14.5 9.1 %copy-start.1 = (f32[4,16,8,128]{3,2,1,0:T(8,128)S(1)}, f32[4,16,8,128]{3,2,1,0:T(8,128)}, u32[]{:S(2)}) copy-start(f32[4,16,8,128]{3,2,1,0:T(8,128)} %param.9) | copy-start | bytes 786436
  17.0 1.2 %collective-permute-start.4 = (f32[16,128]{1,0:T(8,128)S(1)}, f32[16,128]{1,0:T(8,128)S(1)}, u32[]{:S(2)}, u32[]{:S(2)}) collective-permute-start(f32[16,128]{1,0:T(8,128)S(1)} %get-tuple-element.37), channel_id=1, source_target_pairs={{0,16},{1,17},{2,18},{3,19},{4,20},{5,21},{6,22},{7,23},{8,24},{9,... | collective-permute-start | bytes 24584 | tf_op jit(solution)/shard_map/ppermute | solution.py:502
  17.0 3.7 %collective-permute-start.5 = (f32[16,128]{1,0:T(8,128)S(1)}, f32[16,128]{1,0:T(8,128)S(1)}, u32[]{:S(2)}, u32[]{:S(2)}) collective-permute-start(f32[16,128]{1,0:T(8,128)S(1)} %get-tuple-element.38), channel_id=1, source_target_pairs={{0,1},{1,0},{2,3},{3,2},{4,5},{5,4},{6,7},{7,6},{8,9},{9,8},{10,11... | collective-permute-start | bytes 24584 | tf_op jit(solution)/shard_map/ppermute | solution.py:502
  20.7 3.7 %collective-permute-start.6 = (f32[16,128]{1,0:T(8,128)S(1)}, f32[16,128]{1,0:T(8,128)S(1)}, u32[]{:S(2)}, u32[]{:S(2)}) collective-permute-start(f32[16,128]{1,0:T(8,128)S(1)} %get-tuple-element.40), channel_id=1, source_target_pairs={{0,1},{1,0},{2,3},{3,2},{4,5},{5,4},{6,7},{7,6},{8,9},{9,8},{10,11... | collective-permute-start | bytes 24584 | tf_op jit(solution)/shard_map/ppermute | solution.py:502
  20.8 5.8 %collective-permute-start.7 = (f32[16,128]{1,0:T(8,128)S(1)}, f32[16,128]{1,0:T(8,128)S(1)}, u32[]{:S(2)}, u32[]{:S(2)}) collective-permute-start(f32[16,128]{1,0:T(8,128)S(1)} %get-tuple-element.41), channel_id=1, source_target_pairs={{0,16},{1,2},{2,1},{3,4},{4,3},{5,6},{6,5},{7,8},{8,7},{9,10},{10,... | collective-permute-start | bytes 24584 | tf_op jit(solution)/shard_map/ppermute | solution.py:502
  23.6 3.1 %copy-start.7 = (s32[1,9,128]{2,0,1:T(1,128)S(1)}, s32[1,9,128]{2,0,1:T(1,128)}, u32[]{:S(2)}) copy-start(s32[1,9,128]{2,0,1:T(1,128)} %param.17) | copy-start | bytes 13828

commit v4 on v3

--- a/solution.py
+++ b/solution.py
@@ -10,6 +10,7 @@
 I32 = jnp.int32
 
 TILES = 4
+HALF = 64
 SUBSTEPS = 4
 LEV = 16
 BUCKETS = 9
@@ -44,6 +45,10 @@
     )(*args)
 
 
+def in_hbm(x):
+    return pltpu.with_memory_space_constraint(x, pltpu.HBM)
+
+
 def shaped(*shape, dtype=F32):
     return jax.ShapeDtypeStruct(shape, dtype)
 
@@ -92,12 +97,28 @@
     return jnp.concatenate(rows, axis=0)
 
 
-def sample_kernel(ocean_ref, cell_ref, even_ref, odd_ref, own_ref):
+def sample_kernel(
+    ocean_hbm, cell_hbm, even_ref, odd_ref, own_ref, ocean_ref, cell_ref, surface_ref, sems
+):
+    copies = [pltpu.make_async_copy(cell_hbm, cell_ref, sems.at[0])]
+    for f in range(3):
+        copies.append(
+            pltpu.make_async_copy(
+                ocean_hbm.at[pl.ds(f * LEV * 8, 8), :],
+                surface_ref.at[pl.ds(f * 8, 8), :],
+                sems.at[1 + f],
+            )
+        )
+    whole = pltpu.make_async_copy(ocean_hbm, ocean_ref, sems.at[4])
+    for copy in copies:
+        copy.start()
+    whole.start()
+    for copy in copies:
+        copy.wait()
     even = is_even("ocx")
     cells = lanes_row(cell_ref)
     table = one_hot(cells & 127)
-    surface = jnp.concatenate([ocean_ref[pl.ds(f * 128, 8), :] for f in range(3)], axis=0)
-    picked = join3(dot_nn(split3(surface), table))
+    picked = join3(dot_nn(split3(surface_ref[...]), table))
     row_hit = lax.broadcasted_iota(I32, (8, ENTRIES), 0) == jnp.broadcast_to(
         cells >> 7, (8, ENTRIES)
     )
@@ -107,6 +128,7 @@
     ]
     send_both(even, bucket_rows(fields, 2), bucket_rows(fields, 0), even_ref, odd_ref, 0, 9)
     own_ref[pl.ds(0, 9), :] = bucket_rows(fields, 1)
+    whole.wait()
     first = ocean_ref[pl.ds(0, 64, stride=8), :]
     last = ocean_ref[pl.ds(7, 64, stride=8), :]
     send_both(even, last, first, even_ref, odd_ref, 16, 64)
@@ -140,35 +162,41 @@
     )
 
 
+def partners(row):
+    wide = jnp.broadcast_to(row, (8, 128))
+    return jnp.concatenate(
+        [pltpu.roll(wide, 1 + 8 * k, 1, stride=1, stride_axis=0) for k in range(HALF // 8)], axis=0
+    )
+
+
 def pair_forces(x8, v8, reach_ref, contact_ref, bond_ref):
-    turned = jnp.concatenate([x8, v8], axis=0).T
     rows = [[None] * TILES for _ in range(2)]
-    step = 32
-
-    def column(c, lo):
-        return jnp.broadcast_to(turned[lo : lo + step, c : c + 1], (step, 128))
+    flipped = 7 - lax.broadcasted_iota(I32, (8, 128), 0)
 
     def wide(row):
-        return jnp.broadcast_to(row, (step, 128))
+        return jnp.broadcast_to(row, (8, 128))
 
     for t in range(TILES):
-        total_x = jnp.zeros((8, 128), F32)
-        total_y = jnp.zeros((8, 128), F32)
-        for lo in range(0, 128, step):
-            part = pl.ds(lo, step)
-            dx = column(t, lo) - wide(x8[t : t + 1])
-            dy = column(4 + t, lo) - wide(x8[4 + t : 5 + t])
+        own = [wide(src[c + t : c + t + 1]) for src in (x8, v8) for c in (0, 4)]
+        action = [jnp.zeros((8, 128), F32)] * 2
+        reaction = [jnp.zeros((8, 128), F32)] * 2
+        for k in range(HALF // 8):
+            part = pl.ds(8 * k, 8)
+            dx, dy, dvx, dvy = [
+                pltpu.roll(o, 1 + 8 * k, 1, stride=1, stride_axis=0) - o for o in own
+            ]
             depth = jnp.maximum(1.0 - (dx * dx + dy * dy) * reach_ref[t, part, :], 0.0)
             stiff = depth * contact_ref[t, part, :]
             damp = (CONTACT_DAMP / CONTACT_STIFF) * stiff + bond_ref[t, part, :]
-            dvx = column(8 + t, lo) - wide(v8[t : t + 1])
-            dvy = column(12 + t, lo) - wide(v8[4 + t : 5 + t])
-            fx = damp * dvx - stiff * dx
-            fy = damp * dvy - stiff * dy
-            total_x = total_x + jnp.sum(fx.reshape(step // 8, 8, 128), axis=0)
-            total_y = total_y + jnp.sum(fy.reshape(step // 8, 8, 128), axis=0)
-        rows[0][t] = jnp.sum(total_x, axis=0, keepdims=True)
-        rows[1][t] = jnp.sum(total_y, axis=0, keepdims=True)
+            force = (damp * dvx - stiff * dx, damp * dvy - stiff * dy)
+            for c in range(2):
+                action[c] = action[c] + force[c]
+                back = force[c] if k == 0 else pltpu.roll(force[c], 128 - 8 * k, 1)
+                reaction[c] = reaction[c] + back
+        for c in range(2):
+            back = jnp.take_along_axis(reaction[c], flipped, axis=0)
+            back = pltpu.roll(back, 120, 1, stride=1, stride_axis=0)
+            rows[c][t] = jnp.sum(action[c] - back, axis=0, keepdims=True)
     return jnp.concatenate(rows[0] + rows[1], axis=0)
 
 
@@ -181,23 +209,30 @@
 def pair_kernel(
     pairs_ref, bonds_ref, broken_ref, props_ref, state_ref, reach_ref, contact_ref, bond_ref, force_ref
 ):
-    def differences(ref, t, n):
-        ids = lax.broadcasted_iota(I32, (128, n), 0)
+    def differences(ref, t, n, ids):
         first = jnp.broadcast_to(ref[0, pl.ds(t, 1), :], (128, n))
         second = jnp.broadcast_to(ref[1, pl.ds(t, 1), :], (128, n))
         return jnp.where(ids == second, 1.0, 0.0) - jnp.where(ids == first, 1.0, 0.0)
 
+    def by_offset(table, backward):
+        square = dot_nt(table.astype(BF16), backward.astype(BF16))
+        return pltpu.roll(square, 0, 1, stride=1, stride_axis=0).T[:HALF]
+
     radius = tile_rows(props_ref, 0)
-    radius_columns = jnp.concatenate([radius, radius], axis=0).T
+    once = jnp.where(lax.broadcasted_iota(I32, (HALF, 128), 0) == HALF - 1, 0.5, 1.0)
     for t in range(TILES):
-        slots = differences(pairs_ref, t, 512).astype(BF16)
-        contact_ref[t] = -CONTACT_STIFF * dot_nt(slots, slots)
+        ids = lax.broadcasted_iota(I32, (128, 512), 0)
+        table = differences(pairs_ref, t, 512, ids)
+        contact_ref[t] = -CONTACT_STIFF * once * by_offset(
+            table, differences(pairs_ref, t, 512, 127 - ids)
+        )
+        ids = lax.broadcasted_iota(I32, (128, 256), 0)
         alive = jnp.broadcast_to(broken_ref[pl.ds(t, 1), :], (128, 256)) == 0
-        ends = jnp.where(alive, differences(bonds_ref, t, 256), 0.0).astype(BF16)
-        bond_ref[t] = -BOND_DAMP * dot_nt(ends, ends)
-        reach = jnp.broadcast_to(radius_columns[:, t : t + 1], (128, 128)) + jnp.broadcast_to(
-            radius[t : t + 1], (128, 128)
-        )
+        table = jnp.where(alive, differences(bonds_ref, t, 256, ids), 0.0)
+        bond_ref[t] = -BOND_DAMP * once * by_offset(
+            table, differences(bonds_ref, t, 256, 127 - ids)
+        )
+        reach = partners(radius[t : t + 1]) + jnp.broadcast_to(radius[t : t + 1], (HALF, 128))
         reach_ref[t] = 1.0 / (reach * reach)
     x8, v8 = state_rows(state_ref)
     force_ref[...] = pair_forces(x8, v8, reach_ref, contact_ref, bond_ref)
@@ -262,7 +297,7 @@
     force_ref,
     state_ref,
     props_ref,
-    next_ref,
+    moved_ref,
     even_ref,
     odd_ref,
     own_ref,
@@ -294,11 +329,8 @@
         v8 = v8 + push * force
         x8 = x8 + TIME_STEP * v8
         mean = mean + v8 * (1.0 / SUBSTEPS)
-    for k in range(2):
-        for t in range(TILES):
-            lanes = pl.ds(t * 128, 128)
-            next_ref[pl.ds(k, 1), lanes] = x8[4 * k + t : 4 * k + t + 1]
-            next_ref[pl.ds(2 + k, 1), lanes] = v8[4 * k + t : 4 * k + t + 1]
+    moved_ref[pl.ds(0, 8), :] = x8
+    moved_ref[pl.ds(8, 8), :] = v8
     picked = jnp.where(tile_hit, join3(dot_nn(split3(mean), table)), 0.0)
     flux = [
         DRAG_COEF
@@ -313,7 +345,21 @@
     own_ref[pl.ds(0, 12), :] = bucket_rows(flux, 1)
 
 
-def ocean_kernel(ocean_ref, x_even_ref, x_odd_ref, y_even_ref, y_odd_ref, out_ref, low_ref, high_ref):
+def ocean_kernel(
+    ocean_ref,
+    x_even_ref,
+    x_odd_ref,
+    y_even_ref,
+    y_odd_ref,
+    moved_ref,
+    out_ref,
+    next_ref,
+    low_ref,
+    high_ref,
+):
+    for k in range(4):
+        for t in range(TILES):
+            next_ref[pl.ds(k, 1), pl.ds(t * 128, 128)] = moved_ref[pl.ds(4 * k + t, 1), :]
     i, j = lax.axis_index("ocx"), lax.axis_index("ocy")
     x_even, y_even = lax.rem(i, 2) == 0, lax.rem(j, 2) == 0
     rows = pl.ds(16, 64)
@@ -431,9 +477,20 @@
         weight = couple_weight.reshape(BUCKETS, 1, 128)
         cell = couple_cell.reshape(BUCKETS, 1, 128)
         small = shaped(16, 128)
-        send_even, send_odd, own = call(
-            sample_kernel, (shaped(80, 128), shaped(80, 128), small), ocean, cell
-        )
+        block = shaped(4 * LEV * 8, 128)
+        hbm = pl.BlockSpec(memory_space=pltpu.HBM)
+        send_even, send_odd, own, ocean = pl.pallas_call(
+            sample_kernel,
+            out_shape=(shaped(80, 128), shaped(80, 128), small, block),
+            in_specs=[hbm, hbm],
+            out_specs=(VMEM_SPEC,) * 4,
+            scratch_shapes=[
+                pltpu.VMEM((BUCKETS, 1, 128), I32),
+                pltpu.VMEM((24, 128), F32),
+                pltpu.SemaphoreType.DMA((5,)),
+            ],
+            compiler_params=GRANT,
+        )(in_hbm(ocean), in_hbm(cell))
         ge_x = exchange(send_even, x_even)
         go_x = exchange(send_odd, x_odd)
         cols, table, area, salt = call(
@@ -449,7 +506,7 @@
         )
         ge_y = exchange(send_even, y_even)
         go_y = exchange(send_odd, y_odd)
-        square = shaped(TILES, 128, 128)
+        square = shaped(TILES, HALF, 128)
         reach, contact, bond, force = call(
             pair_kernel,
             (square, square, square, shaped(8, 128)),
@@ -459,9 +516,9 @@
             floe_props,
             floe_state,
         )
-        floe_next, send_even, send_odd, own = call(
+        moved, send_even, send_odd, own = call(
             floe_kernel,
-            (shaped(4, 512), small, small, small),
+            (small, small, small, small),
             ge_y,
             go_y,
             keep,
@@ -484,15 +541,15 @@
         )
         he_y = exchange(send_even, y_even)
         ho_y = exchange(send_odd, y_odd)
-        moved = pl.pallas_call(
+        ocean, floe_next = pl.pallas_call(
             ocean_kernel,
-            out_shape=shaped(4 * LEV * 8, 128),
-            in_specs=[VMEM_SPEC] * 5,
-            out_specs=VMEM_SPEC,
+            out_shape=(block, shaped(4, 512)),
+            in_specs=[VMEM_SPEC] * 6,
+            out_specs=(VMEM_SPEC,) * 2,
             scratch_shapes=[pltpu.VMEM((64, 128), F32), pltpu.VMEM((64, 128), F32)],
             compiler_params=GRANT,
-        )(ocean, ge_x, go_x, ge_y, go_y)
-        ocean_next = call(forcing_kernel, shaped(4 * LEV * 8, 128), he_y, ho_y, keep, cell, moved)
+        )(ocean, ge_x, go_x, ge_y, go_y, moved)
+        ocean_next = call(forcing_kernel, block, he_y, ho_y, keep, cell, ocean)
         return (ocean_next.reshape(ocean_state.shape), floe_next)
 
     return body

time: 27.8 us -> 26.3 us (0.946)
  waiting for transfers between devices: 10.2 us -> 8.47 us
  Pallas kernels: 5.32 us -> 7.02 us
  local copies, waits for them, and re-layouts: 1.67 us -> 0.04 us
    ppermute x8, waiting for transfers between devices: 10.2 us -> 8.47 us  [exchange(): return lax.ppermute(data, AXES, pairs)]
    unnamed x22 -> x16, local copies, waits for them, and re-layouts: 1.67 us -> 0.04 us
    pallas_call x1 -> x2, Pallas kernels: 0.49 us -> 2.12 us  [the longest x1 1.09 us: body(): pl.pallas_call(sample_kernel, out_shape=(shaped(80, 128), shaped(80, 128)...]
    pallas_call x7 -> x6, Pallas kernels: 4.82 us -> 4.9 us  [call(): pl.pallas_call(kernel, out_shape=outs, in_specs=[VMEM_SPEC] * len(args),...]
  transfers between devices with their start and end apart: 8 -> 8, of which waited for: 6 -> 5; matrix products, arithmetic and copies ran while one was open for 0% -> 0% of each run, Pallas kernels for 6% -> 13%
where the time goes in v4:
time: 26.3 us; the launch traced here: 26.1 us
  starting transfers between devices  9.82 us (37%)
  waiting for transfers between devices  8.47 us (32%)
  Pallas kernels  7.02 us (27%)
  between operations  0.75 us (3%)
    ppermute x8, starting transfers between devices, exchange(): return lax.ppermute(data, AXES, pairs)  9.82 us
    ppermute x8, waiting for transfers between devices, exchange(): return lax.ppermute(data, AXES, pairs)  8.47 us
    pallas_call x6, Pallas kernels, call(): pl.pallas_call(kernel, out_shape=outs, in_specs=[VMEM_SPEC] * len(args),...  4.9 us
    pallas_call x1, Pallas kernels, body(): pl.pallas_call(sample_kernel, out_shape=(shaped(80, 128), shaped(80, 128)...  1.09 us
    pallas_call x1, Pallas kernels, body(): pl.pallas_call(ocean_kernel, out_shape=(block, shaped(4, 512)), in_specs=...  1.03 us
  transfers between devices with their start and end apart: 8, of which 5 were waited for; matrix products, arithmetic and copies ran while one was open for 0% of the time, Pallas kernels for 13%

profile of v4, /device:TPU:24, one launch (start us, length us, event | category | flops | bytes accessed | tf_op | source)
XLA Modules:
  0.0 26.1 jit_solution(12877418175296891034)
XLA Ops:
  0.6 0.0 copy-start.3
  0.6 1.1 %shard_map.104 = (f32[80,128]{1,0:T(8,128)S(1)}, f32[80,128]{1,0:T(8,128)S(1)}, f32[16,128]{1,0:T(8,128)S(1)}, f32[512,128]{1,0:T(8,128)S(1)}) custom-call(f32[512,128]{1,0:T(8,128)} %bitcast.12, s32[9,1,128]{2,1,0:T(1,128)} %bitcast.9), custom_call_target="tpu_custom_call" | custom-call | tf_op jit(solution)/shard_map/pallas_call | solution.py:482
  1.7 0.0 copy-start.2
  1.7 0.0 copy-start
  1.8 0.1 collective-permute-start
  1.9 2.0 %collective-permute-start.1 = (f32[80,128]{1,0:T(8,128)S(1)}, f32[80,128]{1,0:T(8,128)S(1)}, u32[]{:S(2)}, u32[]{:S(2)}) collective-permute-start(f32[80,128]{1,0:T(8,128)S(1)} %get-tuple-element.27), channel_id=1, source_target_pairs={{0,1},{1,0},{2,3},{3,2},{4,5},{5,4},{6,7},{7,6},{8,9},{9,8},{10,11... | collective-permute-start | bytes 122888 | tf_op jit(solution)/shard_map/ppermute | solution.py:559
  3.9 0.0 copy-done.3
  3.9 0.0 copy-done.2
  3.9 0.0 copy-done
  3.9 0.3 %shard_map.105 = (f32[8,128]{1,0:T(8,128)S(1)}, bf16[128,1152]{1,0:T(8,128)(2,1)S(1)}, f32[8,128]{1,0:T(8,128)S(1)}, f32[1,1152]{1,0:T(1,128)S(1)}) custom-call(f32[512,128]{1,0:T(8,128)S(1)} %get-tuple-element.29.ocean_ref, s32[9,1,128]{2,1,0:T(1,128)S(1)} %bitcast.5, f32[9,1,128]{2,1,0:T(1,128)S(1)} %bitcast.7, f32[2,512]{1,0:T(2,128)S(1)} %copy-done), custom_call_target="tpu_custom_call" | custom-call | bytes 65536 | tf_op jit(solution)/shard_map/pallas_call | solution.py:38
  4.2 0.0 collective-permute-done.refs_0_.x_even_ref
  4.2 1.7 %collective-permute-done.1.refs_1_.x_odd_ref = f32[80,128]{1,0:T(8,128)S(1)} collective-permute-done((f32[80,128]{1,0:T(8,128)S(1)}, f32[80,128]{1,0:T(8,128)S(1)}, u32[]{:S(2)}, u32[]{:S(2)}) %collective-permute-start.1) | collective-permute-done | bytes 40992 | tf_op jit(solution)/shard_map/ppermute | solution.py:559
  5.9 0.0 copy-start.1
  5.9 0.0 copy-start.5
  5.9 0.0 copy-start.6
  5.9 0.0 copy-start.7
  6.0 2.0 %collective-permute-start.2 = (f32[16,128]{1,0:T(8,128)S(1)}, f32[16,128]{1,0:T(8,128)S(1)}, u32[]{:S(2)}, u32[]{:S(2)}) collective-permute-start(f32[16,128]{1,0:T(8,128)S(1)} %get-tuple-element.31), channel_id=1, source_target_pairs={{0,1},{1,0},{2,3},{3,2},{4,5},{5,4},{6,7},{7,6},{8,9},{9,8},{10,11... | collective-permute-start | bytes 24584 | tf_op jit(solution)/shard_map/ppermute | solution.py:559
  8.0 2.7 %collective-permute-start.3 = (f32[16,128]{1,0:T(8,128)S(1)}, f32[16,128]{1,0:T(8,128)S(1)}, u32[]{:S(2)}, u32[]{:S(2)}) collective-permute-start(f32[16,128]{1,0:T(8,128)S(1)} %get-tuple-element.32), channel_id=1, source_target_pairs={{0,16},{1,2},{2,1},{3,4},{4,3},{5,6},{6,5},{7,8},{8,7},{9,10},{10,... | collective-permute-start | bytes 24584 | tf_op jit(solution)/shard_map/ppermute | solution.py:559
  10.7 0.0 copy-done.1
  10.7 0.0 copy-done.5
  10.7 0.0 copy-done.6
  10.7 0.0 copy-done.7
  10.7 2.0 %shard_map.107 = (f32[4,64,128]{2,1,0:T(8,128)S(1)}, f32[4,64,128]{2,1,0:T(8,128)S(1)}, f32[4,64,128]{2,1,0:T(8,128)S(1)}, f32[8,128]{1,0:T(8,128)S(1)}) custom-call(s32[2,4,512]{2,1,0:T(4,128)S(1)} %copy-done.5, s32[2,4,256]{2,1,0:T(4,128)S(1)} %copy-done.6, s32[4,256]{1,0:T(4,128)S(1)} %copy-done.7, f32[2,512]{1,0:T(2,128)S(1)} %copy-done, ...), custom_call_target="tpu_custom_call" | custom-call | bytes 65536 | tf_op jit(solution)/shard_map/pallas_call | solution.py:38
  12.7 0.0 collective-permute-done.2.got_even_ref.y_even_ref
  12.7 1.1 %collective-permute-done.3.got_odd_ref.y_odd_ref = f32[16,128]{1,0:T(8,128)S(1)} collective-permute-done((f32[16,128]{1,0:T(8,128)S(1)}, f32[16,128]{1,0:T(8,128)S(1)}, u32[]{:S(2)}, u32[]{:S(2)}) %collective-permute-start.3) | collective-permute-done | bytes 8224 | tf_op jit(solution)/shard_map/ppermute | solution.py:559
  13.7 1.6 %shard_map.108 = (f32[16,128]{1,0:T(8,128)S(1)}, f32[16,128]{1,0:T(8,128)S(1)}, f32[16,128]{1,0:T(8,128)S(1)}, f32[16,128]{1,0:T(8,128)S(1)}) custom-call(f32[16,128]{1,0:T(8,128)S(1)} %collective-permute-done.2.got_even_ref.y_even_ref, f32[16,128]{1,0:T(8,128)S(1)} %collective-permute-done.3.got_odd_ref.y_odd_ref, ...), custom_call_target="tpu_custom_call" | custom-call | bytes 65536 | tf_op jit(solution)/shard_map/pallas_call | solution.py:38
  15.4 0.1 collective-permute-start.4
  15.4 0.1 collective-permute-start.5
  15.5 1.1 %collective-permute-done.4.refs_0_ = f32[16,128]{1,0:T(8,128)S(1)} collective-permute-done((f32[16,128]{1,0:T(8,128)S(1)}, f32[16,128]{1,0:T(8,128)S(1)}, u32[]{:S(2)}, u32[]{:S(2)}) %collective-permute-start.4) | collective-permute-done | bytes 8224 | tf_op jit(solution)/shard_map/ppermute | solution.py:559
  16.6 2.6 %collective-permute-done.5.refs_1_ = f32[16,128]{1,0:T(8,128)S(1)} collective-permute-done((f32[16,128]{1,0:T(8,128)S(1)}, f32[16,128]{1,0:T(8,128)S(1)}, u32[]{:S(2)}, u32[]{:S(2)}) %collective-permute-start.5) | collective-permute-done | bytes 8224 | tf_op jit(solution)/shard_map/ppermute | solution.py:559
  19.2 0.1 collective-permute-start.6
  19.3 2.8 %collective-permute-start.7 = (f32[16,128]{1,0:T(8,128)S(1)}, f32[16,128]{1,0:T(8,128)S(1)}, u32[]{:S(2)}, u32[]{:S(2)}) collective-permute-start(f32[16,128]{1,0:T(8,128)S(1)} %get-tuple-element.45), channel_id=1, source_target_pairs={{0,16},{1,2},{2,1},{3,4},{4,3},{5,6},{6,5},{7,8},{8,7},{9,10},{10,... | collective-permute-start | bytes 24584 | tf_op jit(solution)/shard_map/ppermute | solution.py:559
  22.1 0.0 copy-start.4
  22.1 1.0 %shard_map.110 = (f32[512,128]{1,0:T(8,128)S(1)}, f32[4,512]{1,0:T(4,128)}) custom-call(f32[512,128]{1,0:T(8,128)S(1)} %get-tuple-element.29.ocean_ref, f32[80,128]{1,0:T(8,128)S(1)} %collective-permute-done.refs_0_.x_even_ref, f32[80,128]{1,0:T(8,128)S(1)} %collective-permute-done.1.refs_1_.x_odd_ref, ...), custom_call_target="tpu_custom_call" | custom-call | tf_op jit(solution)/shard_map/pallas_call | solution.py:544
  23.1 0.0 collective-permute-done.6.got_even_ref
  23.1 2.0 %collective-permute-done.7.got_odd_ref = f32[16,128]{1,0:T(8,128)S(1)} collective-permute-done((f32[16,128]{1,0:T(8,128)S(1)}, f32[16,128]{1,0:T(8,128)S(1)}, u32[]{:S(2)}, u32[]{:S(2)}) %collective-permute-start.7) | collective-permute-done | bytes 8224 | tf_op jit(solution)/shard_map/ppermute | solution.py:559
  25.1 0.0 copy-done.4
  25.1 1.0 %shard_map.111 = f32[512,128]{1,0:T(8,128)} custom-call(f32[16,128]{1,0:T(8,128)S(1)} %collective-permute-done.6.got_even_ref, f32[16,128]{1,0:T(8,128)S(1)} %collective-permute-done.7.got_odd_ref, f32[16,128]{1,0:T(8,128)S(1)} %get-tuple-element.46.keep_ref, s32[9,1,128]{2,1,0:T(1,128)S(1)} %bitcast.10, f32[512,128]{1,0:T(8,128)S(1)} %get-tuple-element.48.ocean_ref), custom_call_target="tpu_custom_call" | custom-call | bytes 65536 | tf_op jit(solution)/shard_map/pallas_call | solution.py:38
  (2 shorter events, 0.0 us)
Async XLA Ops:
  0.6 3.2 %copy-start.3 = (f32[1,9,128]{2,0,1:T(1,128)S(1)}, f32[1,9,128]{2,0,1:T(1,128)}, u32[]{:S(2)}) copy-start(f32[1,9,128]{2,0,1:T(1,128)} %param.16) | copy-start | bytes 13828
  1.7 2.1 %copy-start.2 = (s32[1,9,128]{2,0,1:T(1,128)S(1)}, s32[1,9,128]{2,0,1:T(1,128)}, u32[]{:S(2)}) copy-start(s32[1,9,128]{2,0,1:T(1,128)} %param.15) | copy-start | bytes 13828
  1.7 2.1 %copy-start = (f32[2,512]{1,0:T(2,128)S(1)}, f32[2,512]{1,0:T(2,128)}, u32[]{:S(2)}) copy-start(f32[2,512]{1,0:T(2,128)} %props_ref.5) | copy-start | bytes 12292
  1.8 2.4 %collective-permute-start = (f32[80,128]{1,0:T(8,128)S(1)}, f32[80,128]{1,0:T(8,128)S(1)}, u32[]{:S(2)}, u32[]{:S(2)}) collective-permute-start(f32[80,128]{1,0:T(8,128)S(1)} %get-tuple-element.26), channel_id=1, source_target_pairs={{0,16},{1,17},{2,18},{3,19},{4,20},{5,21},{6,22},{7,23},{8,24},{9,... | collective-permute-start | bytes 122888 | tf_op jit(solution)/shard_map/ppermute | solution.py:559
  1.9 4.1 %collective-permute-start.1 = (f32[80,128]{1,0:T(8,128)S(1)}, f32[80,128]{1,0:T(8,128)S(1)}, u32[]{:S(2)}, u32[]{:S(2)}) collective-permute-start(f32[80,128]{1,0:T(8,128)S(1)} %get-tuple-element.27), channel_id=1, source_target_pairs={{0,1},{1,0},{2,3},{3,2},{4,5},{5,4},{6,7},{7,6},{8,9},{9,8},{10,11... | collective-permute-start | bytes 122888 | tf_op jit(solution)/shard_map/ppermute | solution.py:559
  5.9 4.7 %copy-start.1 = (f32[4,512]{1,0:T(4,128)S(1)}, f32[4,512]{1,0:T(4,128)}, u32[]{:S(2)}) copy-start(f32[4,512]{1,0:T(4,128)} %state_ref.3) | copy-start | bytes 24580
  5.9 4.7 %copy-start.5 = (s32[2,4,512]{2,1,0:T(4,128)S(1)}, s32[2,4,512]{2,1,0:T(4,128)}, u32[]{:S(2)}) copy-start(s32[2,4,512]{2,1,0:T(4,128)} %pairs_ref.1) | copy-start | bytes 49156
  5.9 4.7 %copy-start.6 = (s32[2,4,256]{2,1,0:T(4,128)S(1)}, s32[2,4,256]{2,1,0:T(4,128)}, u32[]{:S(2)}) copy-start(s32[2,4,256]{2,1,0:T(4,128)} %bonds_ref.1) | copy-start | bytes 24580
  5.9 4.7 %copy-start.7 = (s32[4,256]{1,0:T(4,128)S(1)}, s32[4,256]{1,0:T(4,128)}, u32[]{:S(2)}) copy-start(s32[4,256]{1,0:T(4,128)} %broken_ref.1) | copy-start | bytes 12292
  6.0 6.7 %collective-permute-start.2 = (f32[16,128]{1,0:T(8,128)S(1)}, f32[16,128]{1,0:T(8,128)S(1)}, u32[]{:S(2)}, u32[]{:S(2)}) collective-permute-start(f32[16,128]{1,0:T(8,128)S(1)} %get-tuple-element.31), channel_id=1, source_target_pairs={{0,1},{1,0},{2,3},{3,2},{4,5},{5,4},{6,7},{7,6},{8,9},{9,8},{10,11... | collective-permute-start | bytes 24584 | tf_op jit(solution)/shard_map/ppermute | solution.py:559
  8.0 5.8 %collective-permute-start.3 = (f32[16,128]{1,0:T(8,128)S(1)}, f32[16,128]{1,0:T(8,128)S(1)}, u32[]{:S(2)}, u32[]{:S(2)}) collective-permute-start(f32[16,128]{1,0:T(8,128)S(1)} %get-tuple-element.32), channel_id=1, source_target_pairs={{0,16},{1,2},{2,1},{3,4},{4,3},{5,6},{6,5},{7,8},{8,7},{9,10},{10,... | collective-permute-start | bytes 24584 | tf_op jit(solution)/shard_map/ppermute | solution.py:559
  15.4 1.3 %collective-permute-start.4 = (f32[16,128]{1,0:T(8,128)S(1)}, f32[16,128]{1,0:T(8,128)S(1)}, u32[]{:S(2)}, u32[]{:S(2)}) collective-permute-start(f32[16,128]{1,0:T(8,128)S(1)} %get-tuple-element.41), channel_id=1, source_target_pairs={{0,16},{1,17},{2,18},{3,19},{4,20},{5,21},{6,22},{7,23},{8,24},{9,... | collective-permute-start | bytes 24584 | tf_op jit(solution)/shard_map/ppermute | solution.py:559
  15.4 3.7 %collective-permute-start.5 = (f32[16,128]{1,0:T(8,128)S(1)}, f32[16,128]{1,0:T(8,128)S(1)}, u32[]{:S(2)}, u32[]{:S(2)}) collective-permute-start(f32[16,128]{1,0:T(8,128)S(1)} %get-tuple-element.42), channel_id=1, source_target_pairs={{0,1},{1,0},{2,3},{3,2},{4,5},{5,4},{6,7},{7,6},{8,9},{9,8},{10,11... | collective-permute-start | bytes 24584 | tf_op jit(solution)/shard_map/ppermute | solution.py:559
  19.2 3.9 %collective-permute-start.6 = (f32[16,128]{1,0:T(8,128)S(1)}, f32[16,128]{1,0:T(8,128)S(1)}, u32[]{:S(2)}, u32[]{:S(2)}) collective-permute-start(f32[16,128]{1,0:T(8,128)S(1)} %get-tuple-element.44), channel_id=1, source_target_pairs={{0,1},{1,0},{2,3},{3,2},{4,5},{5,4},{6,7},{7,6},{8,9},{9,8},{10,11... | collective-permute-start | bytes 24584 | tf_op jit(solution)/shard_map/ppermute | solution.py:559
  19.3 5.8 %collective-permute-start.7 = (f32[16,128]{1,0:T(8,128)S(1)}, f32[16,128]{1,0:T(8,128)S(1)}, u32[]{:S(2)}, u32[]{:S(2)}) collective-permute-start(f32[16,128]{1,0:T(8,128)S(1)} %get-tuple-element.45), channel_id=1, source_target_pairs={{0,16},{1,2},{2,1},{3,4},{4,3},{5,6},{6,5},{7,8},{8,7},{9,10},{10,... | collective-permute-start | bytes 24584 | tf_op jit(solution)/shard_map/ppermute | solution.py:559
  22.1 3.1 %copy-start.4 = (s32[1,9,128]{2,0,1:T(1,128)S(1)}, s32[1,9,128]{2,0,1:T(1,128)}, u32[]{:S(2)}) copy-start(s32[1,9,128]{2,0,1:T(1,128)} %param.17) | copy-start | bytes 13828
